TPU v7x, 128 devices: a whole 4x4x4 slice. The times are simulated.
128 devices in a mesh: grp: 8 (over y, core), lane: 16 (over x, z).
Axes of the slice: x: 4, y: 4, z: 4, core: 2. Of those that a mesh axis runs over, the one named last changes fastest.
Arguments:
- fine_in: bfloat16 [2, 2048, 16, 256], P(None, ('grp', 'lane')), may hold values from -6 to 6
- counts: int32 [2, 128], P(None, ('grp', 'lane')), may hold values from 1 to 15, as said below
- neighbour_refs: int32 [2, 2048, 16], P(None, ('grp', 'lane')), may hold values from 0 to 271, as said below
- offset_codes: int32 [2, 2048, 16], P(None, ('grp', 'lane')), may hold values from 0 to 26, as said below
- neighbour_mask: int32 [2, 2048, 16], P(None, ('grp', 'lane')), may hold values 0 or 1
- send_slots: int32 [2, 128, 256], P(None, ('grp', 'lane')), may hold values from 0 to 14, as said below
- parent_of: int32 [2048], P(('grp', 'lane')), may hold values from -1 to 15, as said below
- child_code: int32 [2048], P(('grp', 'lane')), may hold values from 0 to 7, as said below
- coarse_refs: int32 [128, 16], P(('grp', 'lane')), may hold values from 0 to 127
- coarse_codes: int32 [128, 16], P(('grp', 'lane')), may hold values from 0 to 26, as said below
- coarse_mask: int32 [128, 16], P(('grp', 'lane')), may hold values 0 or 1
- ops_x: bfloat16 [3, 4, 3, 16, 16], replicated, may hold values from -0.75 to 0.75
- ops_y: bfloat16 [3, 4, 3, 16, 16], replicated, may hold values from -0.75 to 0.75
- ops_z: bfloat16 [3, 4, 3, 16, 16], replicated, may hold values from -0.75 to 0.75
- filters: bfloat16 [2, 16, 16], replicated, may hold values from -1.5 to 1.5
Outputs:
- fine_out: bfloat16 [2, 2048, 16, 256], P(None, ('grp', 'lane'))
- coarse_out: bfloat16 [128, 16, 256], P(('grp', 'lane'))
Inputs may be any that keep to these rules, and one draw needn't show every extreme that they name: The counts of the devices of one grp index add up to 128 on level 1. send_slots[l, q, r * 2 + c] is a live slot of device q on level l. `neighbour_refs`: A value below 16 is a live slot of the block's own device; a larger one is 16 + q * 2 + c, entry c of what device q sends to the block's device. `offset_codes`: the codes of one block are distinct. `coarse_codes`: the codes of one coarse block are distinct. `parent_of`: -1 exactly on slots that are not live on level 1; every coarse block of a subtree has 8 live children there, one of each child code. `child_code`: 0 on slots that are not live.
All inputs are finite; a program needn't handle non-finite values. No bound on the sum of `neighbour_mask` or of `coarse_mask` on one device may be relied on, other than what follows from the above.
Results may differ from a plain program's by a relative error of at most 0.0088.
Values may be sent and summed in bfloat16 or wider, within the bound.
No kernel may reach another device: no remote copies, remote signals or barrier semaphores. Data moves between devices by JAX's collectives and lax.ppermute only.
A program may use at most 256 MiB of HBM per device.

v0:
```python
import jax
import jax.numpy as jnp
from jax import lax
from jax.sharding import PartitionSpec as P

offset_total = 27


def outer_tables(left_ops, right_ops):
    term_count = left_ops.shape[0]
    left_count = left_ops.shape[1]
    right_count = right_ops.shape[1]
    order_size = left_ops.shape[-1]
    left_flat = jnp.transpose(left_ops, (0, 1, 3, 2)).reshape(
        term_count, left_count * order_size * order_size
    )
    right_flat = jnp.transpose(right_ops, (0, 1, 3, 2)).reshape(
        term_count, right_count * order_size * order_size
    )
    outer = jnp.matmul(
        left_flat[:, :, None], right_flat[:, None, :], preferred_element_type=jnp.float32
    ).astype(jnp.bfloat16)
    outer = outer.reshape(
        term_count, left_count, order_size, order_size, right_count, order_size, order_size
    )
    return jnp.transpose(outer, (0, 1, 4, 2, 5, 3, 6))


def stacked_tables(left_ops, right_ops):
    order_size = left_ops.shape[-1]
    return outer_tables(left_ops, right_ops).reshape(-1, order_size * order_size)


def kron_tables(left_ops, right_ops):
    order_size = left_ops.shape[-1]
    arranged = outer_tables(left_ops, right_ops).reshape(
        -1, order_size * order_size, order_size * order_size
    )
    return jnp.transpose(arranged, (0, 2, 1))


def row_matrix(row_ops):
    order_size = row_ops.shape[-1]
    arranged = jnp.transpose(row_ops, (2, 0, 1, 3))
    return arranged.reshape(order_size * row_ops.shape[0], 3 * order_size)


def apply_blocks(source_blocks, offset_codes, neighbour_mask, row_matrix_ops, flat_tables):
    row_count = source_blocks.shape[0]
    slot_count = source_blocks.shape[1]
    order_size = source_blocks.shape[2]
    hits = (
        offset_codes[:, None, :] == jnp.arange(offset_total, dtype=jnp.int32)[None, :, None]
    ) & (neighbour_mask[:, None, :] == 1)
    slot_index = jnp.sum(
        jnp.where(hits, jnp.arange(slot_count, dtype=jnp.int32)[None, None, :], 0), axis=2
    )
    present = jnp.any(hits, axis=2)
    picked = jnp.take_along_axis(source_blocks, slot_index[:, :, None, None], axis=1)
    grouped = jnp.where(present[:, :, None, None], picked, jnp.zeros_like(picked))
    grouped = grouped.reshape(row_count, 3, 9, order_size, order_size * order_size)
    grouped = jnp.transpose(grouped, (0, 1, 3, 2, 4)).reshape(
        row_count, 3 * order_size, 9 * order_size * order_size
    )
    spread = jnp.matmul(row_matrix_ops, grouped, preferred_element_type=jnp.float32).astype(
        jnp.bfloat16
    )
    spread = spread.reshape(row_count * order_size, -1)
    result = jnp.dot(spread, flat_tables, preferred_element_type=jnp.float32)
    return result.reshape(row_count, order_size, order_size * order_size)


def corner_sum(lifted_rows, filter_tables, corner, transpose):
    block_count = corner.shape[0]
    running = jnp.zeros(lifted_rows.shape, jnp.float32)
    for corner_index in range(4):
        filter_table = filter_tables[corner_index].T if transpose else filter_tables[corner_index]
        product = jnp.dot(lifted_rows, filter_table, preferred_element_type=jnp.float32)
        chosen = jnp.repeat(corner == corner_index, lifted_rows.shape[0] // block_count)[:, None]
        running = running + jnp.where(chosen, product, jnp.zeros_like(product))
    return running.reshape(block_count, -1, lifted_rows.shape[1])


def route_blocks(outgoing):
    return lax.all_to_all(outgoing, ("grp", "lane"), split_axis=0, concat_axis=0, tiled=True)


def fine_level(
    blocks,
    live_count,
    neighbour_refs,
    offset_codes,
    neighbour_mask,
    send_slots,
    row_matrix_ops,
    flat_tables,
):
    slot_total = blocks.shape[0]
    live_mask = jnp.arange(slot_total, dtype=jnp.int32) < live_count
    masked = jnp.where(live_mask[:, None, None], blocks, jnp.zeros_like(blocks))
    outgoing = jnp.take(masked, send_slots, axis=0)
    arrived = route_blocks(outgoing)
    block_pool = jnp.concatenate([masked, arrived], axis=0)
    source_blocks = jnp.take(block_pool, neighbour_refs, axis=0)
    result = apply_blocks(source_blocks, offset_codes, neighbour_mask, row_matrix_ops, flat_tables)
    return (jnp.where(live_mask[:, None, None], result, jnp.zeros_like(result)), masked)


def body(
    fine_in,
    counts,
    neighbour_refs,
    offset_codes,
    neighbour_mask,
    send_slots,
    parent_of,
    child_code,
    coarse_refs,
    coarse_codes,
    coarse_mask,
    ops_x,
    ops_y,
    ops_z,
    filters,
):
    order_size = filters.shape[1]
    fine_terms = []
    masked_levels = []
    for level_index in range(2):
        flat_tables = stacked_tables(ops_y[level_index], ops_z[level_index])
        result, masked = fine_level(
            fine_in[level_index],
            counts[level_index, 0],
            neighbour_refs[level_index],
            offset_codes[level_index],
            neighbour_mask[level_index],
            send_slots[level_index, 0],
            row_matrix(ops_x[level_index]),
            flat_tables,
        )
        fine_terms.append(result)
        masked_levels.append(masked)
    filter_tables = kron_tables(filters[None], filters[None])
    upper_bit = child_code // 4
    corner = child_code % 4
    lower_lift = jnp.matmul(filters[0], masked_levels[1], preferred_element_type=jnp.float32)
    upper_lift = jnp.matmul(filters[1], masked_levels[1], preferred_element_type=jnp.float32)
    lifted = jnp.where((upper_bit == 0)[:, None, None], lower_lift, upper_lift).astype(jnp.bfloat16)
    sibling_term = corner_sum(
        lifted.reshape(-1, order_size * order_size), filter_tables, corner, True
    )
    term_rows = sibling_term.reshape(sibling_term.shape[0], -1)
    parent_picks = (
        parent_of[None, :]
        == jnp.arange(lax.axis_size("lane") * coarse_refs.shape[0], dtype=jnp.int32)[:, None]
    ).astype(jnp.float32)
    own_parents = lax.psum_scatter(
        jnp.dot(
            parent_picks,
            term_rows,
            precision=lax.Precision.HIGHEST,
            preferred_element_type=jnp.float32,
        ),
        "lane",
        scatter_dimension=0,
        tiled=True,
    )
    coarse_mine = own_parents.reshape(-1, order_size, order_size * order_size).astype(jnp.bfloat16)
    all_parents = lax.all_gather(coarse_mine, ("grp", "lane"), axis=0, tiled=True)
    coarse_flat = stacked_tables(ops_y[2], ops_z[2])
    coarse_out = apply_blocks(
        jnp.take(all_parents, coarse_refs, axis=0),
        coarse_codes,
        coarse_mask,
        row_matrix(ops_x[2]),
        coarse_flat,
    ).astype(jnp.bfloat16)
    group_parents = lax.all_gather(coarse_out, "lane", axis=0, tiled=True)
    parent_picks = (
        parent_of[:, None] == jnp.arange(group_parents.shape[0], dtype=jnp.int32)[None, :]
    ).astype(jnp.bfloat16)
    picked = jnp.dot(
        parent_picks,
        group_parents.reshape(group_parents.shape[0], -1),
        preferred_element_type=jnp.float32,
    ).astype(jnp.bfloat16)
    picked = picked.reshape(masked_levels[1].shape)
    lower_drop = jnp.matmul(filters[0].T, picked, preferred_element_type=jnp.float32)
    upper_drop = jnp.matmul(filters[1].T, picked, preferred_element_type=jnp.float32)
    lowered = jnp.where((upper_bit == 0)[:, None, None], lower_drop, upper_drop).astype(
        jnp.bfloat16
    )
    correction = corner_sum(
        lowered.reshape(-1, order_size * order_size), filter_tables, corner, False
    )
    fine_one = fine_terms[1] + correction
    fine_out = jnp.stack([fine_terms[0], fine_one]).astype(jnp.bfloat16)
    return (fine_out, coarse_out)


def solution(mesh):
    in_specs = (
        P(None, ("grp", "lane"), None, None),
        P(None, ("grp", "lane")),
        P(None, ("grp", "lane"), None),
        P(None, ("grp", "lane"), None),
        P(None, ("grp", "lane"), None),
        P(None, ("grp", "lane"), None),
        P(("grp", "lane")),
        P(("grp", "lane")),
        P(("grp", "lane"), None),
        P(("grp", "lane"), None),
        P(("grp", "lane"), None),
        P(),
        P(),
        P(),
        P(),
    )
    out_specs = (P(None, ("grp", "lane"), None, None), P(("grp", "lane"), None, None))
    return jax.shard_map(body, mesh=mesh, in_specs=in_specs, out_specs=out_specs, check_vma=False)
```

profile of v0, /device:TPU:1, one launch (start us, length us, event | category | flops | bytes accessed | tf_op | source)
XLA Modules:
  0.0 610.8 jit_solution(2309949601464642559)
XLA Ops:
  7.2 1.3 fusion.49
  9.5 4.5 reshape.489
  14.0 6.9 %copy.92 = bf16[1,2,2,16,16,16,16]{6,5,4,3,2,1,0:T(8,128)(2,1)} copy(bf16[1,2,2,16,16,16,16]{6,4,2,5,3,1,0:T(8,128)(2,1)} %bitcast.244) | data formatting | bytes 1048576 | tf_op jit(solution)/shard_map/transpose | solution.py:26
  20.9 5.5 reshape.490
  29.5 64.6 %all-reduce.2 = bf16[16,4096]{1,0:T(8,128)(2,1)S(1)} all-reduce(f32[16,4096]{1,0:T(8,128)S(1)} %fusion.31), channel_id=3, replica_groups=mesh['grp'=8,'lane'=16] {'lane'}, use_global_device_ids=true, to_apply=%region_6.10.clone | all-reduce | flops 65536 | bytes 393216
  96.9 0.8 gather_fusion.5
  97.8 2.0 broadcast_select_fusion
  99.7 20.8 %all-to-all-start.1 = ((bf16[256,16,256]{2,1,0:T(8,128)(2,1)}), bf16[256,16,256]{2,1,0:T(8,128)(2,1)}, u32[]{:S(2)}, u32[]{:S(2)}) async-start(bf16[256,16,256]{2,1,0:T(8,128)(2,1)} %broadcast_select_fusion), calls=%async_computation.1 | async-start | bytes 4194304 | tf_op jit(solution)/shard_map/all_to_all | solution.py:85
  124.4 0.8 gather_fusion.2
  125.2 0.8 fusion.21
  126.1 1.9 broadcast_select_fusion.1
  128.0 2.8 multiply_convert_fusion
  130.8 2.9 multiply_convert_fusion.1
  133.6 2.8 multiply_convert_fusion.2
  137.2 37.2 %reshape.498 = bf16[4,3,16,16,3,16,16]{6,5,4,3,2,1,0:T(8,128)(2,1)} reshape(bf16[4,768,768]{2,1,0:T(8,128)(2,1)} %multiply_convert_fusion) | data formatting | bytes 9437184 | tf_op jit(solution)/shard_map/reshape | solution.py:23
  174.5 26.2 %copy.97 = bf16[4,3,3,16,16,16,16]{6,5,4,3,2,1,0:T(8,128)(2,1)} copy(bf16[4,3,3,16,16,16,16]{6,4,2,5,3,1,0:T(8,128)(2,1)} %bitcast.241) | data formatting | bytes 9437184 | tf_op jit(solution)/shard_map/transpose | solution.py:26
  200.7 44.5 %reshape.499 = bf16[9216,256]{1,0:T(8,128)(2,1)} reshape(bf16[4,3,3,16,16,16,16]{6,5,4,3,2,1,0:T(8,128)(2,1)} %copy.97) | data formatting | bytes 9437184 | tf_op jit(solution)/shard_map/reshape | solution.py:31
  245.4 37.2 %reshape.484 = bf16[4,3,16,16,3,16,16]{6,5,4,3,2,1,0:T(8,128)(2,1)} reshape(bf16[4,768,768]{2,1,0:T(8,128)(2,1)} %multiply_convert_fusion.1) | data formatting | bytes 9437184 | tf_op jit(solution)/shard_map/reshape | solution.py:23
  282.6 25.9 %copy.90 = bf16[4,3,3,16,16,16,16]{6,5,4,3,2,1,0:T(8,128)(2,1)} copy(bf16[4,3,3,16,16,16,16]{6,4,2,5,3,1,0:T(8,128)(2,1)} %bitcast.242) | data formatting | bytes 9437184 | tf_op jit(solution)/shard_map/transpose | solution.py:26
  308.5 44.5 %reshape.626 = bf16[9216,256,1]{1,0,2:T(8,128)(2,1)} reshape(bf16[4,3,3,16,16,16,16]{6,5,4,3,2,1,0:T(8,128)(2,1)} %copy.90) | data formatting | bytes 9437184 | tf_op jit(solution)/shard_map/reshape | solution.py:31
  353.2 49.8 %reshape.475 = bf16[4,3,16,16,3,16,16]{6,5,4,3,2,1,0:T(8,128)(2,1)} reshape(bf16[4,768,768]{2,1,0:T(8,128)(2,1)} %multiply_convert_fusion.2) | data formatting | bytes 9437184 | tf_op jit(solution)/shard_map/reshape | solution.py:23
  402.9 25.9 %copy.84 = bf16[4,3,3,16,16,16,16]{6,5,4,3,2,1,0:T(8,128)(2,1)} copy(bf16[4,3,3,16,16,16,16]{6,4,2,5,3,1,0:T(8,128)(2,1)} %bitcast.243) | data formatting | bytes 9437184 | tf_op jit(solution)/shard_map/transpose | solution.py:26
  428.8 44.5 %reshape.624 = bf16[9216,256,1]{1,0,2:T(8,128)(2,1)} reshape(bf16[4,3,3,16,16,16,16]{6,5,4,3,2,1,0:T(8,128)(2,1)} %copy.84) | data formatting | bytes 9437184 | tf_op jit(solution)/shard_map/reshape | solution.py:31
  473.3 1.8 gather_fusion
  476.5 3.1 convolution_convert_fusion.4
  479.6 18.5 %all-gather = bf16[256,256]{1,0:T(8,128)(2,1)S(1)} all-gather(bf16[16,256]{1,0:T(8,128)(2,1)S(1)} %convolution_convert_fusion.4), channel_id=2, replica_groups=mesh['grp'=8,'lane'=16] {'lane'}, dimensions={0}, use_global_device_ids=true | all-gather | bytes 139264 | tf_op jit(solution)/shard_map/all_gather | solution.py:178
  499.2 13.2 %all-to-all-start = ((bf16[256,16,256]{2,1,0:T(8,128)(2,1)}), bf16[256,16,256]{2,1,0:T(8,128)(2,1)}, u32[]{:S(2)}, u32[]{:S(2)}) async-start(bf16[256,16,256]{2,1,0:T(8,128)(2,1)} %broadcast_select_fusion.1), calls=%async_computation | async-start | bytes 4194304 | tf_op jit(solution)/shard_map/all_to_all | solution.py:85
  512.9 0.9 fusion.3
  513.8 1.8 pad_maximum_fusion.1
  515.6 2.1 gather_fusion.6
  517.7 1.8 broadcast_select_fusion.2
  519.5 5.6 gather_fusion.7
  525.1 3.3 select_select_fusion
  528.4 5.0 copy.85
  533.4 8.3 %reshape.478 = bf16[16,48,2304]{2,1,0:T(8,128)(2,1)} reshape(bf16[16,3,16,9,256]{4,3,2,1,0:T(8,128)(2,1)} %copy.85) | data formatting | bytes 7077888 | tf_op jit(solution)/shard_map/reshape | solution.py:62
  541.7 5.5 fusion.1
  547.2 8.3 %dot_general.99 = bf16[16,16,9216]{2,1,0:T(8,128)(2,1)} reshape(bf16[16,64,2304]{2,1,0:T(8,128)(2,1)} %fusion.1) | data formatting | bytes 9437184 | tf_op jit(solution)/shard_map/dot_general | solution.py:69
  555.5 1.8 pad_maximum_fusion
  557.3 2.1 gather_fusion.3
  559.4 1.8 broadcast_select_fusion.3
  561.2 5.6 gather_fusion.4
  566.8 3.3 select_select_fusion.1
  570.2 5.0 copy.79
  575.1 6.9 %reshape.469 = bf16[16,48,2304]{2,1,0:T(8,128)(2,1)S(1)} reshape(bf16[16,3,16,9,256]{4,3,2,1,0:T(8,128)(2,1)} %copy.79) | data formatting | bytes 7077888 | tf_op jit(solution)/shard_map/reshape | solution.py:62
  582.1 3.5 fusion
  585.5 8.4 %dot_general.93 = bf16[16,16,9216]{2,1,0:T(8,128)(2,1)} reshape(bf16[16,64,2304]{2,1,0:T(8,128)(2,1)} %fusion) | data formatting | bytes 9437184 | tf_op jit(solution)/shard_map/dot_general | solution.py:69
  593.9 5.3 fusion.15
  599.3 3.7 fusion.14
  (177 shorter events, 15.2 us)
Async XLA Ops:
  7.2 466.1 %all-gather.3.cloned.1.call-start = ((), (), s32[]{:S(2)}) async-start(), calls=%async_computation.2 | async-start | bytes 1056768 | tf_op jit(solution)/shard_map/all_gather | solution.py:169
  20.9 5.6 copy-start.28
  20.9 7.0 %copy-start.2 = (bf16[2,16,16,256]{3,2,1,0:T(8,128)(2,1)S(1)}, bf16[2,16,16,256]{3,2,1,0:T(8,128)(2,1)}, u32[]{:S(2)}) copy-start(bf16[2,16,16,256]{3,2,1,0:T(8,128)(2,1)} %param.21) | copy-start | bytes 786436
  20.9 7.0 %copy-start.9 = (bf16[2,16,16]{2,1,0:T(8,128)(2,1)S(1)}, bf16[2,16,16]{2,1,0:T(8,128)(2,1)}, u32[]{:S(2)}) copy-start(bf16[2,16,16]{2,1,0:T(8,128)(2,1)} %param.35) | copy-start | bytes 3076
  20.9 8.3 %copy-start.24 = (s32[16]{0:T(128)S(1)}, s32[16]{0:T(128)}, u32[]{:S(2)}) copy-start(s32[16]{0:T(128)} %param.27) | copy-start | bytes 196
  26.5 67.6 %copy-start.34 = (u32[128]{0:T(128)S(1)}, u32[128]{0:T(128)}, u32[]{:S(2)}) copy-start(u32[128]{0:T(128)} %constant.152) | copy-start | bytes 1540
  26.5 69.6 %copy-start.25 = (s32[2,1,256]{2,1,0:T(1,128)S(1)}, s32[2,1,256]{2,1,0:T(1,128)}, u32[]{:S(2)}) copy-start(s32[2,1,256]{2,1,0:T(1,128)} %param.26) | copy-start | bytes 6148
  27.2 70.5 %copy-start.26 = (pred[16]{0:T(512)(128)(4,1)}, pred[16]{0:T(512)(128)(4,1)S(1)}, u32[]{:S(2)}) copy-start(pred[16]{0:T(512)(128)(4,1)S(1)} %get-tuple-element.34) | copy-start | bytes 52
  27.5 70.1 %copy-start.18 = (pred[256]{0:T(512)(128)(4,1)}, pred[256]{0:T(512)(128)(4,1)S(1)}, u32[]{:S(2)}) copy-start(pred[256]{0:T(512)(128)(4,1)S(1)} %broadcast_in_dim.243) | copy-start | bytes 772
  27.7 70.0 %copy-start.20 = (pred[256]{0:T(512)(128)(4,1)}, pred[256]{0:T(512)(128)(4,1)S(1)}, u32[]{:S(2)}) copy-start(pred[256]{0:T(512)(128)(4,1)S(1)} %broadcast_in_dim.246) | copy-start | bytes 772
  27.9 69.8 %copy-start.22 = (pred[256]{0:T(512)(128)(4,1)}, pred[256]{0:T(512)(128)(4,1)S(1)}, u32[]{:S(2)}) copy-start(pred[256]{0:T(512)(128)(4,1)S(1)} %broadcast_in_dim.249) | copy-start | bytes 772
  96.7 3.0 copy-start.29
  96.9 27.6 %copy-start = (bf16[16,16,256]{2,1,0:T(8,128)(2,1)}, bf16[16,16,256]{2,1,0:T(8,128)(2,1)S(1)}, u32[]{:S(2)}) copy-start(bf16[16,16,256]{2,1,0:T(8,128)(2,1)S(1)} %get-tuple-element.7) | copy-start | bytes 393220
  97.7 22.8 %copy-start.31 = (s32[1,16]{1,0:T(1,128)S(1)}, s32[1,16]{1,0:T(1,128)}, u32[]{:S(2)}) copy-start(s32[1,16]{1,0:T(1,128)} %param.29) | copy-start | bytes 196
  97.7 22.9 %copy-start.32 = (s32[1,16]{1,0:T(1,128)S(1)}, s32[1,16]{1,0:T(1,128)}, u32[]{:S(2)}) copy-start(s32[1,16]{1,0:T(1,128)} %param.31) | copy-start | bytes 196
  97.7 22.9 %copy-start.33 = (s32[1,16]{1,0:T(1,128)S(1)}, s32[1,16]{1,0:T(1,128)}, u32[]{:S(2)}) copy-start(s32[1,16]{1,0:T(1,128)} %param.30) | copy-start | bytes 196
  97.7 23.1 %copy-start.7 = (s32[2,16,16]{2,1,0:T(8,128)S(1)}, s32[2,16,16]{2,1,0:T(8,128)}, u32[]{:S(2)}) copy-start(s32[2,16,16]{2,1,0:T(8,128)} %param.23) | copy-start | bytes 6148
  97.7 23.7 %copy-start.12 = (s32[2,16,16]{2,1,0:T(8,128)S(1)}, s32[2,16,16]{2,1,0:T(8,128)}, u32[]{:S(2)}) copy-start(s32[2,16,16]{2,1,0:T(8,128)} %param.24) | copy-start | bytes 6148
  97.8 23.7 %copy-start.11 = (s32[2,16,16]{2,1,0:T(8,128)S(1)}, s32[2,16,16]{2,1,0:T(8,128)}, u32[]{:S(2)}) copy-start(s32[2,16,16]{2,1,0:T(8,128)} %param.25) | copy-start | bytes 6148
  97.8 24.6 %copy-start.4 = (bf16[3,4,3,16,16]{4,3,2,1,0:T(8,128)(2,1)S(1)}, bf16[3,4,3,16,16]{4,3,2,1,0:T(8,128)(2,1)}, u32[]{:S(2)}) copy-start(bf16[3,4,3,16,16]{4,3,2,1,0:T(8,128)(2,1)} %param.33) | copy-start | bytes 55300
  97.8 24.7 %copy-start.5 = (bf16[3,4,3,16,16]{4,3,2,1,0:T(8,128)(2,1)S(1)}, bf16[3,4,3,16,16]{4,3,2,1,0:T(8,128)(2,1)}, u32[]{:S(2)}) copy-start(bf16[3,4,3,16,16]{4,3,2,1,0:T(8,128)(2,1)} %param.34) | copy-start | bytes 55300
  99.7 399.4 %all-to-all-start.1 = ((bf16[256,16,256]{2,1,0:T(8,128)(2,1)}), bf16[256,16,256]{2,1,0:T(8,128)(2,1)}, u32[]{:S(2)}, u32[]{:S(2)}) async-start(bf16[256,16,256]{2,1,0:T(8,128)(2,1)} %broadcast_select_fusion), calls=%async_computation.1 | async-start | bytes 4194304 | tf_op jit(solution)/shard_map/all_to_all | solution.py:85
  121.7 4.3 copy-start.6
  479.6 33.0 %copy-start.10 = (bf16[16,256]{1,0:T(8,128)(2,1)}, bf16[16,256]{1,0:T(8,128)(2,1)S(1)}, u32[]{:S(2)}) copy-start(bf16[16,256]{1,0:T(8,128)(2,1)S(1)} %convolution_convert_fusion.4) | copy-start | bytes 24580
  479.6 32.8 %copy-start.19 = (pred[256]{0:T(512)(128)(4,1)S(1)}, pred[256]{0:T(512)(128)(4,1)}, u32[]{:S(2)}) copy-start(pred[256]{0:T(512)(128)(4,1)} %copy-done.18) | copy-start | bytes 772
  479.6 33.0 %copy-start.21 = (pred[256]{0:T(512)(128)(4,1)S(1)}, pred[256]{0:T(512)(128)(4,1)}, u32[]{:S(2)}) copy-start(pred[256]{0:T(512)(128)(4,1)} %copy-done.20) | copy-start | bytes 772
  498.4 14.4 %copy-start.23 = (pred[256]{0:T(512)(128)(4,1)S(1)}, pred[256]{0:T(512)(128)(4,1)}, u32[]{:S(2)}) copy-start(pred[256]{0:T(512)(128)(4,1)} %copy-done.22) | copy-start | bytes 772
  499.2 56.4 %all-to-all-start = ((bf16[256,16,256]{2,1,0:T(8,128)(2,1)}), bf16[256,16,256]{2,1,0:T(8,128)(2,1)}, u32[]{:S(2)}, u32[]{:S(2)}) async-start(bf16[256,16,256]{2,1,0:T(8,128)(2,1)} %broadcast_select_fusion.1), calls=%async_computation | async-start | bytes 4194304 | tf_op jit(solution)/shard_map/all_to_all | solution.py:85
  519.5 5.6 copy-start.15
  519.5 5.6 copy-start.17
  547.2 8.3 %copy-start.1 = (bf16[16,16,256]{2,1,0:T(8,128)(2,1)S(1)}, bf16[16,16,256]{2,1,0:T(8,128)(2,1)}, u32[]{:S(2)}) copy-start(bf16[16,16,256]{2,1,0:T(8,128)(2,1)} %copy-done) | copy-start | bytes 393220
  555.5 1.8 copy-start.8
  555.5 3.9 copy-start.13
  561.2 5.6 copy-start.14
  561.2 5.6 copy-start.16
  585.5 8.4 %copy-start.30 = (pred[16]{0:T(512)(128)(4,1)S(1)}, pred[16]{0:T(512)(128)(4,1)}, u32[]{:S(2)}) copy-start(pred[16]{0:T(512)(128)(4,1)} %copy-done.29) | copy-start | bytes 52
  585.5 13.7 %slice-start = ((s8[4718592]{0:T(1024)(128)(4,1)}), s8[524288]{0:T(1024)(128)(4,1)S(1)}, s32[]{:S(2)}) async-start(s8[4718592]{0:T(1024)(128)(4,1)} %bitcast.259), calls=%async_computation.3 | async-start | bytes 1048576
  593.9 5.3 slice-start.1
  593.9 5.3 copy-start.3
  593.9 5.3 copy-start.27
Sparse Core Ops, SparseCore 0:
  96.2 87.0 all-gather.2
where the time goes:
time: 619 us; the launch traced here: 611 us
  local copies, waits for them, and re-layouts  420 us (68%)
  blocking collectives  83.1 us (13%)
  starting transfers between devices  34 us (5%)
  other arithmetic  33 us (5%)
  matrix products  25 us (4%)
  between operations  15.3 us (2%)
    reshape x3, local copies, waits for them, and re-layouts, stacked_tables(): outer_tables(left_ops, right_ops).reshape(-1, order_size * order_size)  133 us
    reshape x4, local copies, waits for them, and re-layouts, outer_tables(): outer.reshape(term_count, left_count, order_size, order_size, right_count...  129 us
    transpose x4, local copies, waits for them, and re-layouts, outer_tables(): return jnp.transpose(outer, (0, 1, 4, 2, 5, 3, 6))  84.9 us
    unnamed x1, blocking collectives  64.6 us
    all_to_all x2, starting transfers between devices, route_blocks(): lax.all_to_all(outgoing, ('grp', 'lane'), split_axis=0, concat_axis=0, ti...  34 us
    all_gather x1, blocking collectives, body(): group_parents = lax.all_gather(coarse_out, 'lane', axis=0, tiled=True)  18.5 us
    dot_general x2, local copies, waits for them, and re-layouts, apply_blocks(): result = jnp.dot(spread, flat_tables, preferred_element_type=jnp.float32)  16.7 us
    reshape x2, local copies, waits for them, and re-layouts, apply_blocks(): jnp.transpose(grouped, (0, 1, 3, 2, 4))  15.2 us
  transfers between devices with their start and end apart: 3, of which 0 were waited for; matrix products, arithmetic and copies ran while one was open for 67% of the time, Pallas kernels for 0%

commit v1 on v0

v1 whole, which is shorter than its diff:
```python
import jax
import jax.numpy as jnp
from jax import lax
from jax.experimental import pallas as pl
from jax.experimental.pallas import tpu as pltpu
from jax.sharding import PartitionSpec as P

K = 16
KK = K * K
TERMS = 4
SLOT = 16
CAP = 2
CODES = 27
BF = jnp.bfloat16
F32 = jnp.float32
AXES = ("grp", "lane")


def iota(shape, dim):
    return lax.broadcasted_iota(jnp.int32, shape, dim)


def spreads():
    row, col = iota((K, KK), 0), iota((K, KK), 1)
    return (col // K == row).astype(BF), (col % K == row).astype(BF)


def dot(a, b):
    return jnp.dot(a, b, preferred_element_type=F32)


def corner_tables(rep, tile):
    rows = []
    for cy in range(2):
        for cz in range(2):
            for p in range(K):
                rows.append((rep[cy][p : p + 1, :] * tile[cz]).astype(BF))
    return jnp.concatenate(rows, axis=0)


def corner_spread(blocks, code_ref):
    columns = []
    for corner in range(4):
        rows = []
        for b in range(SLOT):
            part = blocks[b * K : (b + 1) * K, :]
            rows.append(jnp.where(code_ref[b] % 4 == corner, part, jnp.zeros_like(part)))
        columns.append(jnp.concatenate(rows, axis=0))
    return jnp.concatenate(columns, axis=1)


def lift_kernel(parent_ref, code_ref, x_ref, filt_ref, filt_t_ref, info_ref, out_ref, acc_ref):
    repeat, tiled = spreads()
    tile_n = [dot(filt_ref[c], tiled) for c in range(2)]
    rep_t = [dot(filt_t_ref[c], repeat) for c in range(2)]
    tile_t = [dot(filt_t_ref[c], tiled) for c in range(2)]
    lane_block = iota((K, KK), 1) // K
    rows = []
    for b in range(SLOT):
        chosen = jnp.where(code_ref[b] // 4 == 1, tile_n[1], tile_n[0])
        rows.append(jnp.where(lane_block == b, chosen, 0.0).astype(BF))
    lifted = dot(jnp.concatenate(rows, axis=0), x_ref[0].reshape(SLOT * K, KK)).astype(BF)
    moved = dot(corner_spread(lifted, code_ref), corner_tables(rep_t, tile_t))
    acc_ref[...] = jnp.zeros_like(acc_ref)
    for b in range(SLOT):
        parent = parent_ref[b]
        target = jnp.where(parent < 0, SLOT, parent)
        acc_ref[target] = acc_ref[target] + moved[b * K : (b + 1) * K, :]
    for t in range(SLOT):
        out_ref[t, 0:K, :] = acc_ref[t].astype(BF)
        out_ref[t, K : K + 8, :] = info_ref[...]


def gather_kernel(slots_ref, fine_ref, out_ref):
    step = pl.program_id(0)
    for r in range(16):
        for level in range(2):
            for c in range(CAP):
                slot = slots_ref[level * 256 + (step * 16 + r) * CAP + c]
                out_ref[r, level * CAP + c] = fine_ref[level, slot]


def place_kernel(recv_ref, send_in_ref, send_ref, copies_ref, sem):
    total = recv_ref[0, 0:K, :].astype(F32)
    for lane in range(1, 16):
        total = total + recv_ref[lane, 0:K, :].astype(F32)
    mine = total.astype(BF)
    for r in range(128):
        copies_ref[r] = mine
    copy = pltpu.make_async_copy(copies_ref, send_ref.at[:, 4], sem)
    copy.start()
    copy.wait()


def tail_kernel(
    idx_ref,
    parent_ref,
    code_ref,
    place_ref,
    arrived_ref,
    fine_ref,
    xbd_ref,
    yw_ref,
    zw_ref,
    filt_ref,
    filt_t_ref,
    fine_out_ref,
    coarse_out_ref,
    pool_ref,
    spread_ref,
    table_ref,
    acc_ref,
    coarse_ref,
    sems,
):
    copies = [
        pltpu.make_async_copy(fine_ref.at[0], pool_ref.at[128:144, 0], sems.at[0]),
        pltpu.make_async_copy(arrived_ref.at[:, 0:2], pool_ref.at[0:128, 0:2], sems.at[1]),
        pltpu.make_async_copy(fine_ref.at[1], pool_ref.at[128:144, 1], sems.at[2]),
        pltpu.make_async_copy(arrived_ref.at[:, 2:4], pool_ref.at[0:128, 2:4], sems.at[3]),
        pltpu.make_async_copy(arrived_ref.at[:, 4], pool_ref.at[0:128, 4], sems.at[4]),
    ]
    for copy in copies:
        copy.start()
    pool_ref[144, 0] = jnp.zeros((K, KK), BF)

    def apply_level(level):
        xbd = xbd_ref[level]
        acc_ref[...] = jnp.zeros_like(acc_ref)

        def step(cyz, carry):
            cy = cyz // 3
            cz = cyz % 3
            for g4 in range(4):
                parts = []
                for b4 in range(4):
                    for cx in range(3):
                        v = idx_ref[(level * SLOT + g4 * 4 + b4) * CODES + 9 * cx + cyz]
                        parts.append(pool_ref[v // 8, v % 8])
                spread = dot(xbd, jnp.concatenate(parts, axis=0)).astype(BF)
                for m in range(TERMS):
                    spread_ref[g4 * 64 : (g4 + 1) * 64, m * KK : (m + 1) * KK] = spread[
                        m * 64 : (m + 1) * 64, :
                    ]
            for m in range(TERMS):
                zpart = zw_ref[level, m * 3 + cz]
                ypart = yw_ref[level, m * 3 + cy]
                for r in range(K):
                    table_ref[m * KK + r * K : m * KK + (r + 1) * K, :] = (
                        ypart[r : r + 1, :] * zpart
                    ).astype(BF)
            acc_ref[...] += dot(spread_ref[...], table_ref[...])
            return carry

        lax.fori_loop(0, 9, step, 0)

    for level in range(2):
        copies[2 * level].wait()
        copies[2 * level + 1].wait()
        apply_level(level)
        for b in range(SLOT):
            live = b < place_ref[level]
            rows = acc_ref[b * K : (b + 1) * K, :]
            rows = jnp.where(live, rows, 0.0)
            if level == 0:
                fine_out_ref[0, b] = rows.astype(BF)
            else:
                coarse_ref[1, b] = rows
    copies[4].wait()
    apply_level(2)
    for t in range(SLOT):
        coarse_ref[0, t] = acc_ref[t * K : (t + 1) * K, :]
    coarse_out_ref[0] = coarse_ref[0, place_ref[2]].astype(BF)

    repeat, tiled = spreads()
    rep_n = [dot(filt_ref[c], repeat) for c in range(2)]
    tile_n = [dot(filt_ref[c], tiled) for c in range(2)]
    tile_t = [dot(filt_t_ref[c], tiled) for c in range(2)]
    lane_block = iota((K, KK), 1) // K
    rows = []
    for b in range(SLOT):
        chosen = jnp.where(code_ref[b] // 4 == 1, tile_t[1], tile_t[0])
        rows.append(jnp.where(lane_block == parent_ref[b], chosen, 0.0).astype(BF))
    lowered = dot(jnp.concatenate(rows, axis=0), acc_ref[...].astype(BF)).astype(BF)
    correction = dot(corner_spread(lowered, code_ref), corner_tables(rep_n, tile_n))
    for b in range(SLOT):
        fine_out_ref[1, b] = (coarse_ref[1, b] + correction[b * K : (b + 1) * K, :]).astype(BF)


def smem():
    return pl.BlockSpec(memory_space=pltpu.SMEM)


def vmem():
    return pl.BlockSpec(memory_space=pltpu.VMEM)


def anywhere():
    return pl.BlockSpec(memory_space=pl.ANY)


def code_index(codes, mask, places, empty):
    hits = (codes[:, None, :] == jnp.arange(CODES, dtype=jnp.int32)[None, :, None]) & (
        mask[:, None, :] == 1
    )
    return empty + jnp.sum(jnp.where(hits, places[:, None, :] - empty, 0), axis=2)


def body(
    fine_in,
    counts,
    neighbour_refs,
    offset_codes,
    neighbour_mask,
    send_slots,
    parent_of,
    child_code,
    coarse_refs,
    coarse_codes,
    coarse_mask,
    ops_x,
    ops_y,
    ops_z,
    filters,
):
    filters_t = jnp.swapaxes(filters, 1, 2)
    info = jnp.concatenate([coarse_refs, coarse_codes, coarse_mask], axis=0).astype(BF)
    info = jnp.pad(info, ((0, 5), (0, KK - 16)))
    partial = pl.pallas_call(
        lift_kernel,
        grid=(1,),
        in_specs=[
            smem(),
            smem(),
            pl.BlockSpec((1, SLOT, K, KK), lambda i: (1, 0, 0, 0)),
            vmem(),
            vmem(),
            vmem(),
        ],
        out_specs=vmem(),
        out_shape=jax.ShapeDtypeStruct((16, K + 8, KK), BF),
        scratch_shapes=[pltpu.VMEM((SLOT + 1, K, KK), F32)],
        name="lift",
    )(parent_of, child_code, fine_in, filters, filters_t, info)
    recv = lax.all_to_all(partial, "lane", split_axis=0, concat_axis=0, tiled=True)

    send = pl.pallas_call(
        gather_kernel,
        grid=(8,),
        in_specs=[smem(), vmem()],
        out_specs=pl.BlockSpec((16, 5, K, KK), lambda i: (i, 0, 0, 0)),
        out_shape=jax.ShapeDtypeStruct((128, 5, K, KK), BF),
        name="gather",
        cost_estimate=pl.CostEstimate(flops=1000, bytes_accessed=9_000_000, transcendentals=0),
    )(send_slots.reshape(512), fine_in)
    send = pl.pallas_call(
        place_kernel,
        in_specs=[vmem(), anywhere()],
        out_specs=anywhere(),
        out_shape=jax.ShapeDtypeStruct((128, 5, K, KK), BF),
        scratch_shapes=[pltpu.VMEM((128, K, KK), BF), pltpu.SemaphoreType.DMA],
        input_output_aliases={1: 0},
        name="place",
    )(recv, send)
    arrived = lax.all_to_all(send, AXES, split_axis=0, concat_axis=0, tiled=True)

    repeat, tiled = spreads()
    yw = jnp.einsum("lmcpr,pk->lmcrk", ops_y, repeat, preferred_element_type=F32)
    zw = jnp.einsum("lmcqs,qk->lmcsk", ops_z, tiled, preferred_element_type=F32)
    yw = yw.reshape(3, 12, K, KK)
    zw = zw.reshape(3, 12, K, KK)
    xm = jnp.transpose(ops_x, (0, 1, 3, 2, 4)).reshape(3, 64, 48)
    row, col = iota((256, 64), 0), iota((256, 64), 1)
    grow = ((row // 64 == col // 16) & (row % 16 == col % 16)).astype(BF)
    row, col = iota((48, 192), 0), iota((48, 192), 1)
    wide = (col % 48 == row).astype(BF)
    row, col = iota((256, 192), 0), iota((256, 192), 1)
    own = (row // 16) % 4 == col // 48
    xbd = jnp.einsum("ij,ljk->lik", grow, xm)
    xbd = jnp.einsum("lik,kn->lin", xbd, wide)
    xbd = jnp.where(own[None], xbd, jnp.zeros_like(xbd))

    empty = 144 * 8
    tables = []
    for level in range(2):
        refs = neighbour_refs[level]
        far = refs - SLOT
        places = jnp.where(
            refs < SLOT, (128 + refs) * 8 + level, (far // CAP) * 8 + CAP * level + far % CAP
        )
        tables.append(code_index(offset_codes[level], neighbour_mask[level], places, empty))
    lists = recv[:, K : K + 3, 0:16].astype(jnp.int32)
    tables.append(code_index(lists[:, 1], lists[:, 2], lists[:, 0] * 8 + 4, empty))
    idx = jnp.concatenate([t.reshape(-1) for t in tables])
    place = jnp.concatenate(
        [counts[:, 0], lax.axis_index("lane").astype(jnp.int32).reshape(1)]
    )

    fine_out, coarse_out = pl.pallas_call(
        tail_kernel,
        in_specs=[smem()] * 4 + [anywhere()] * 2 + [vmem()] * 5,
        out_specs=[vmem(), vmem()],
        out_shape=[
            jax.ShapeDtypeStruct((2, SLOT, K, KK), BF),
            jax.ShapeDtypeStruct((1, K, KK), BF),
        ],
        scratch_shapes=[
            pltpu.VMEM((145, 5, K, KK), BF),
            pltpu.VMEM((KK, TERMS * KK), BF),
            pltpu.VMEM((TERMS * KK, KK), BF),
            pltpu.VMEM((KK, KK), F32),
            pltpu.VMEM((2, SLOT, K, KK), F32),
            pltpu.SemaphoreType.DMA((5,)),
        ],
        name="tail",
    )(
        idx,
        parent_of,
        child_code,
        place,
        arrived,
        fine_in,
        xbd,
        yw,
        zw,
        filters,
        filters_t,
    )
    return fine_out, coarse_out


def solution(mesh):
    blocks = P(None, AXES, None, None)
    table = P(None, AXES, None)
    in_specs = (
        blocks,
        P(None, AXES),
        table,
        table,
        table,
        table,
        P(AXES),
        P(AXES),
        P(AXES, None),
        P(AXES, None),
        P(AXES, None),
        P(),
        P(),
        P(),
        P(),
    )
    out_specs = (blocks, P(AXES, None, None))
    return jax.shard_map(body, mesh=mesh, in_specs=in_specs, out_specs=out_specs, check_vma=False)
```

time: 619 us -> 124 us (0.20); the launches traced: 611 us -> 123 us
  local copies, waits for them, and re-layouts: 420 us -> 3.35 us
  blocking collectives: 83.1 us -> 0 us
  waiting for transfers between devices: 0.02 us -> 58.4 us
  Pallas kernels: 0 us -> 35.2 us
  other arithmetic: 33 us -> 4.8 us
  matrix products: 25 us -> 3.51 us
  starting transfers between devices: 34 us -> 17 us
  between operations: 15.3 us -> 0.92 us
    reshape x15 -> x1, local copies, waits for them, and re-layouts: 283 us -> 0.13 us  [body(): xm = jnp.transpose(ops_x, (0, 1, 3, 2, 4)).reshape(3, 64, 48)]
    transpose x11 -> x1, local copies, waits for them, and re-layouts: 95 us -> 0.14 us  [body(): xm = jnp.transpose(ops_x, (0, 1, 3, 2, 4)).reshape(3, 64, 48)]
    unnamed x1 -> x0, blocking collectives: 64.6 us -> none
    all_to_all x2, waiting for transfers between devices: 0.01 us -> 58.4 us  [the longest x1 56.3 us: body(): lax.all_to_all(send, AXES, split_axis=0, concat_axis=0, tiled=True)]
    pallas_call x0 -> x4, Pallas kernels: none -> 35.2 us  [the longest x1 25.8 us: body(): pl.pallas_call(tail_kernel, in_specs=[smem()] * 4 + [anywhere()] * 2 + [v...]
    dot_general x20 -> x3, matrix products: 25 us -> 3.25 us  [the longest x1 1.1 us: body(): jnp.einsum('lmcpr,pk->lmcrk', ops_y, repeat, preferred_element_type=F32)]
    gather x10 -> x0, local copies, waits for them, and re-layouts: 19.4 us -> none  [the longest x5 11.9 us: apply_blocks(): jnp.take_along_axis(source_blocks, slot_index[:, :, None, None], axis=1)]
    all_gather x1 -> x0, blocking collectives: 18.5 us -> none  [body(): group_parents = lax.all_gather(coarse_out, 'lane', axis=0, tiled=True)]
  transfers between devices with their start and end apart: 3 -> 2, of which waited for: 0 -> 2; matrix products, arithmetic and copies ran while one was open for 67% -> 6% of each run, Pallas kernels for 0% -> 4%
where the time goes in v1:
time: 124 us; the launch traced here: 123 us
  waiting for transfers between devices  58.4 us (47%)
  Pallas kernels  35.2 us (28%)
  starting transfers between devices  17 us (14%)
  other arithmetic  4.8 us (4%)
  matrix products  3.51 us (3%)
  local copies, waits for them, and re-layouts  3.35 us (3%)
    all_to_all x1, waiting for transfers between devices, body(): lax.all_to_all(send, AXES, split_axis=0, concat_axis=0, tiled=True)  56.3 us
    pallas_call x1, Pallas kernels, body(): pl.pallas_call(tail_kernel, in_specs=[smem()] * 4 + [anywhere()] * 2 + [v...  25.8 us
    all_to_all x1, starting transfers between devices, body(): lax.all_to_all(send, AXES, split_axis=0, concat_axis=0, tiled=True)  8.54 us
    all_to_all x1, starting transfers between devices, body(): lax.all_to_all(partial, 'lane', split_axis=0, concat_axis=0, tiled=True)  8.45 us
    pallas_call x1, Pallas kernels, body(): pl.pallas_call(gather_kernel, grid=(8,), in_specs=[smem(), vmem()], out_s...  5.01 us
  transfers between devices with their start and end apart: 2, of which 2 were waited for; matrix products, arithmetic and copies ran while one was open for 6% of the time, Pallas kernels for 4%

profile of v1, /device:TPU:1, one launch (start us, length us, event | category | flops | bytes accessed | tf_op | source)
XLA Modules:
  0.0 123.2 jit_solution(11411918830891384428)
XLA Ops:
  0.6 0.0 copy-start
  0.6 1.4 %copy.27 = bf16[2,16,16]{1,2,0:T(8,128)(2,1)} copy(bf16[2,16,16]{2,1,0:T(8,128)(2,1)} %filt_ref.3) | data formatting | bytes 2048 | tf_op args[14]
  2.0 0.7 convert.11
  2.7 0.7 convert.10
  3.4 0.7 convert.9
  4.0 0.6 fusion.67.info_ref
  4.6 2.2 %lift.1 = bf16[16,24,256]{2,1,0:T(8,128)(2,1)} custom-call(s32[16]{0:T(128)} %parent_ref.3, s32[16]{0:T(128)} %code_ref.3, bf16[2,16,16,256]{3,2,1,0:T(8,128)(2,1)} %fine_ref.3, bf16[2,16,16]{2,1,0:T(8,128)(2,1)} %filt_ref.3, bf16[2,16,16]{2,1,0:T(8,128)(2,1)} %bitcast.100, bf16[8,256]{1,0:T(8,128)(2,1)} %fusion.67.info_ref), custom_call_target="tpu_custom_call" | custom-call | tf_op jit(solution)/shard_map/lift/pallas_call | solution.py:229
  6.9 8.4 %all-to-all-start = ((bf16[16,24,256]{2,1,0:T(8,128)(2,1)}), bf16[16,24,256]{2,1,0:T(8,128)(2,1)S(1)}, u32[]{:S(2)}, u32[]{:S(2)}) async-start(bf16[16,24,256]{2,1,0:T(8,128)(2,1)} %lift.1), calls=%async_computation | async-start | bytes 393216 | tf_op jit(solution)/shard_map/all_to_all | solution.py:245
  15.3 5.0 %gather.1.send_in_ref = bf16[128,5,16,256]{3,2,1,0:T(8,128)(2,1)} custom-call(s32[512]{0:T(512)} %bitcast.106, bf16[2,16,16,256]{3,2,1,0:T(8,128)(2,1)} %fine_ref.3), custom_call_target="tpu_custom_call" | custom-call | flops 1000 | bytes 9000000 | tf_op jit(solution)/shard_map/gather/pallas_call | solution.py:247
  20.3 2.1 %all-to-all-done.recv_ref = bf16[16,24,256]{2,1,0:T(8,128)(2,1)S(1)} async-done(((bf16[16,24,256]{2,1,0:T(8,128)(2,1)}), bf16[16,24,256]{2,1,0:T(8,128)(2,1)S(1)}, u32[]{:S(2)}, u32[]{:S(2)}) %all-to-all-start) | async-done | bytes 196640 | tf_op jit(solution)/shard_map/all_to_all | solution.py:245
  22.5 0.0 copy-start.1
  22.5 0.7 copy-done.1
  23.1 2.2 %place.1 = bf16[128,5,16,256]{3,2,1,0:T(8,128)(2,1)} custom-call(bf16[16,24,256]{2,1,0:T(8,128)(2,1)} %copy-done.1, bf16[128,5,16,256]{3,2,1,0:T(8,128)(2,1)} %gather.1.send_in_ref), custom_call_target="tpu_custom_call", output_to_operand_aliasing={{}: (1, {})} | custom-call | tf_op jit(solution)/shard_map/place/pallas_call | solution.py:256
  25.3 0.0 copy-start.4
  25.3 0.0 copy-start.5
  25.3 0.0 copy-start.6
  25.3 0.0 copy-start.3
  25.4 0.0 copy-start.7
  25.4 0.0 copy-start.2
  25.4 8.5 %all-to-all-start.1 = ((bf16[128,5,16,256]{3,2,1,0:T(8,128)(2,1)}), bf16[128,5,16,256]{3,2,1,0:T(8,128)(2,1)}, u32[]{:S(2)}, u32[]{:S(2)}) async-start(bf16[128,5,16,256]{3,2,1,0:T(8,128)(2,1)} %place.1), calls=%async_computation.1 | async-start | bytes 10485760 | tf_op jit(solution)/shard_map/all_to_all | solution.py:265
  33.9 0.0 copy-done.4
  34.0 0.0 copy-done.5
  34.0 0.0 copy-done.6
  34.0 0.3 select_reduce_fusion.1
  34.3 0.1 add.182
  34.4 0.1 add.190
  34.5 0.0 copy-done.3
  34.5 0.1 copy.28
  34.7 0.1 reshape.253
  34.9 0.0 copy-done.7
  34.9 0.7 pad_add_fusion.place_ref
  35.6 0.2 fusion
  35.8 0.3 fusion.6
  36.1 1.0 convolution_select_fusion.xbd_ref
  37.1 0.0 copy-done
  37.1 1.1 fusion.26
  38.2 0.0 copy-done.2
  38.2 1.1 fusion.29
  39.3 0.8 slice_convert_fusion
  40.1 0.2 select_reduce_fusion
  40.3 0.1 add.192
  40.4 0.7 concatenate.11.idx_ref
  41.1 56.3 %all-to-all-done.1.arrived_ref = bf16[128,5,16,256]{3,2,1,0:T(8,128)(2,1)} async-done(((bf16[128,5,16,256]{3,2,1,0:T(8,128)(2,1)}), bf16[128,5,16,256]{3,2,1,0:T(8,128)(2,1)}, u32[]{:S(2)}, u32[]{:S(2)}) %all-to-all-start.1) | async-done | bytes 5242912 | tf_op jit(solution)/shard_map/all_to_all | solution.py:265
  97.4 25.8 %tail.1 = (bf16[2,16,16,256]{3,2,1,0:T(8,128)(2,1)}, bf16[1,16,256]{2,1,0:T(8,128)(2,1)}) custom-call(s32[1296]{0:T(1024)} %concatenate.11.idx_ref, s32[16]{0:T(128)} %parent_ref.3, s32[16]{0:T(128)} %code_ref.3, s32[3]{0:T(128)} %pad_add_fusion.place_ref, bf16[128,5,16,256]{3,2,1,0:T(8,128)(2,1)} %all-to-all-done.1.arrived_ref, ...), custom_call_target="tpu_custom_call" | custom-call | tf_op jit(solution)/shard_map/tail/pallas_call | solution.py:299
  (21 shorter events, 0.2 us)
Async XLA Ops:
  0.6 36.5 %copy-start = (bf16[3,4,3,16,16]{4,3,2,1,0:T(8,128)(2,1)S(1)}, bf16[3,4,3,16,16]{4,3,2,1,0:T(8,128)(2,1)}, u32[]{:S(2)}) copy-start(bf16[3,4,3,16,16]{4,3,2,1,0:T(8,128)(2,1)} %param.27) | copy-start | bytes 55300
  6.9 15.6 %all-to-all-start = ((bf16[16,24,256]{2,1,0:T(8,128)(2,1)}), bf16[16,24,256]{2,1,0:T(8,128)(2,1)S(1)}, u32[]{:S(2)}, u32[]{:S(2)}) async-start(bf16[16,24,256]{2,1,0:T(8,128)(2,1)} %lift.1), calls=%async_computation | async-start | bytes 393216 | tf_op jit(solution)/shard_map/all_to_all | solution.py:245
  22.5 0.7 copy-start.1
  25.3 8.6 %copy-start.4 = (s32[2,16,16]{2,1,0:T(8,128)S(1)}, s32[2,16,16]{2,1,0:T(8,128)}, u32[]{:S(2)}) copy-start(s32[2,16,16]{2,1,0:T(8,128)} %param.19) | copy-start | bytes 6148
  25.3 8.6 %copy-start.5 = (s32[2,16,16]{2,1,0:T(8,128)S(1)}, s32[2,16,16]{2,1,0:T(8,128)}, u32[]{:S(2)}) copy-start(s32[2,16,16]{2,1,0:T(8,128)} %param.17) | copy-start | bytes 6148
  25.3 8.7 %copy-start.6 = (s32[2,16,16]{2,1,0:T(8,128)S(1)}, s32[2,16,16]{2,1,0:T(8,128)}, u32[]{:S(2)}) copy-start(s32[2,16,16]{2,1,0:T(8,128)} %param.18) | copy-start | bytes 6148
  25.3 9.2 %copy-start.3 = (bf16[3,4,3,16,16]{4,3,2,1,0:T(8,128)(2,1)S(1)}, bf16[3,4,3,16,16]{4,3,2,1,0:T(8,128)(2,1)}, u32[]{:S(2)}) copy-start(bf16[3,4,3,16,16]{4,3,2,1,0:T(8,128)(2,1)} %param.26) | copy-start | bytes 55300
  25.4 9.5 %copy-start.7 = (s32[2,1]{0,1:T(1,128)S(1)}, s32[2,1]{0,1:T(1,128)}, u32[]{:S(2)}) copy-start(s32[2,1]{0,1:T(1,128)} %param.16) | copy-start | bytes 28
  25.4 12.8 %copy-start.2 = (bf16[3,4,3,16,16]{4,3,2,1,0:T(8,128)(2,1)S(1)}, bf16[3,4,3,16,16]{4,3,2,1,0:T(8,128)(2,1)}, u32[]{:S(2)}) copy-start(bf16[3,4,3,16,16]{4,3,2,1,0:T(8,128)(2,1)} %param.28) | copy-start | bytes 55300
  25.4 72.0 %all-to-all-start.1 = ((bf16[128,5,16,256]{3,2,1,0:T(8,128)(2,1)}), bf16[128,5,16,256]{3,2,1,0:T(8,128)(2,1)}, u32[]{:S(2)}, u32[]{:S(2)}) async-start(bf16[128,5,16,256]{3,2,1,0:T(8,128)(2,1)} %place.1), calls=%async_computation.1 | async-start | bytes 10485760 | tf_op jit(solution)/shard_map/all_to_all | solution.py:265

commit v2 on v1

v2 whole, which is shorter than its diff:
```python
import jax
import jax.numpy as jnp
from jax import lax
from jax.experimental import pallas as pl
from jax.experimental.pallas import tpu as pltpu
from jax.sharding import PartitionSpec as P

K = 16
KK = K * K
TERMS = 4
SLOT = 16
CAP = 2
CODES = 27
BF = jnp.bfloat16
F32 = jnp.float32
AXES = ("grp", "lane")


def iota(shape, dim):
    return lax.broadcasted_iota(jnp.int32, shape, dim)


def spreads():
    row, col = iota((K, KK), 0), iota((K, KK), 1)
    return (col // K == row).astype(BF), (col % K == row).astype(BF)


def dot(a, b):
    return jnp.dot(a, b, preferred_element_type=F32)


def corner_tables(rep, tile):
    rows = []
    for cy in range(2):
        for cz in range(2):
            for p in range(K):
                rows.append((rep[cy][p : p + 1, :] * tile[cz]).astype(BF))
    return jnp.concatenate(rows, axis=0)


def corner_spread(blocks, code_ref):
    columns = []
    for corner in range(4):
        rows = []
        for b in range(SLOT):
            part = blocks[b * K : (b + 1) * K, :]
            rows.append(jnp.where(code_ref[b] % 4 == corner, part, jnp.zeros_like(part)))
        columns.append(jnp.concatenate(rows, axis=0))
    return jnp.concatenate(columns, axis=1)


def factors(filt_ref):
    repeat, tiled = spreads()
    flip = lambda f, e: lax.dot_general(f, e, (((0,), (0,)), ((), ())), preferred_element_type=F32)
    filts = [filt_ref[c] for c in range(2)]
    rep_n = [dot(f, repeat) for f in filts]
    tile_n = [dot(f, tiled) for f in filts]
    rep_t = [flip(f, repeat) for f in filts]
    tile_t = [flip(f, tiled) for f in filts]
    return rep_n, tile_n, rep_t, tile_t


def send_kernel(
    parent_ref,
    code_ref,
    slots_ref,
    grp_ref,
    fine_ref,
    filt_ref,
    refs_ref,
    codes_ref,
    mask_ref,
    send_ref,
    pack_ref,
    piece_ref,
    acc_ref,
    sems,
):
    copies = []
    for chunk in range(4):
        def fill(r, carry):
            for level in range(2):
                for c in range(CAP):
                    slot = slots_ref[level, 0, r * CAP + c]
                    at = 32 * (level * CAP + c)
                    block = fine_ref[level, slot]
                    pack_ref[r, at : at + 16, :] = block[:, 0:128]
                    pack_ref[r, at + 16 : at + 32, :] = block[:, 128:256]
            return carry

        lax.fori_loop(chunk * 32, chunk * 32 + 32, fill, 0, unroll=4)
        here = pl.ds(chunk * 32, 32)
        copies.append(
            pltpu.make_async_copy(
                pack_ref.at[here], send_ref.at[here, pl.ds(0, 128)], sems.at[chunk]
            )
        )
        copies[-1].start()

    _, tile_n, rep_t, tile_t = factors(filt_ref)
    lane_block = iota((K, KK), 1) // K
    rows = []
    for b in range(SLOT):
        chosen = jnp.where(code_ref[b] // 4 == 1, tile_n[1], tile_n[0])
        rows.append(jnp.where(lane_block == b, chosen, 0.0).astype(BF))
    lifted = dot(jnp.concatenate(rows, axis=0), fine_ref[1].reshape(SLOT * K, KK)).astype(BF)
    moved = dot(corner_spread(lifted, code_ref), corner_tables(rep_t, tile_t))
    parity = grp_ref[0] % 2
    info = jnp.concatenate([refs_ref[...], codes_ref[...]] + [mask_ref[...]] * 6, axis=0)
    wide = (iota((16, 128), 0) == iota((16, 128), 1)).astype(BF)
    info = dot(info.astype(F32).astype(BF), wide).astype(BF)
    for gp in range(4):
        for lane in range(16):
            piece_ref[(2 * gp + parity) * 16 + lane] = info
    acc_ref[...] = jnp.zeros_like(acc_ref)
    for b in range(SLOT):
        parent = parent_ref[b]
        target = jnp.where(parent < 0, SLOT, parent)
        acc_ref[target] = acc_ref[target] + moved[b * K : (b + 1) * K, :]
    for t in range(SLOT):
        for half in range(2):
            for top in range(2):
                tile = acc_ref[t, top * 8 : top * 8 + 8, half * 128 : half * 128 + 128].astype(BF)
                j = t * 4 + half * 2 + top
                piece_ref[(2 * (j // 16) + 1 - parity) * 16 + j % 16] = tile
    copies.append(
        pltpu.make_async_copy(piece_ref, send_ref.at[:, pl.ds(128, 8)], sems.at[4])
    )
    copies[-1].start()
    for copy in copies:
        copy.wait()


def place_kernel(grp_ref, arrived_ref, out_ref, info_ref, piece_ref, sem):
    parity = grp_ref[0] % 2
    copy = pltpu.make_async_copy(arrived_ref.at[:, :, :, pl.ds(128, 8)], piece_ref, sem)
    copy.start()
    copy.wait()
    sums = []
    for g in range(4):
        total = piece_ref[g, 1 - parity, 0].astype(F32)
        for lane in range(1, 16):
            total = total + piece_ref[g, 1 - parity, lane].astype(F32)
        sums.append(total)
    mine = jnp.concatenate(sums, axis=0).astype(BF)
    for r in range(128):
        out_ref[r] = mine
    info_ref[...] = piece_ref[grp_ref[0] // 2, parity]


def apply_level(level, blocks, place, xbd_ref, yw_ref, zw_ref, spread_ref, table_ref, acc_ref):
    xbd = xbd_ref[level]

    def prepare(cyz):
        cy, cz, slot = cyz // 3, cyz % 3, cyz % 2
        for g4 in range(4):
            parts = []
            for b4 in range(4):
                for cx in range(3):
                    at = pl.multiple_of(place(g4 * 4 + b4, 9 * cx + cyz), 32)
                    parts.append(
                        jnp.concatenate(
                            [blocks[pl.ds(at, 16), :], blocks[pl.ds(at + 16, 16), :]], axis=1
                        )
                    )
            spread = dot(xbd, jnp.concatenate(parts, axis=0)).astype(BF)
            for m in range(TERMS):
                spread_ref[slot, g4 * 64 : (g4 + 1) * 64, m * KK : (m + 1) * KK] = spread[
                    m * 64 : (m + 1) * 64, :
                ]
        for m in range(TERMS):
            zpart = zw_ref[level, m * 3 + cz]
            ypart = yw_ref[level, m * 3 + cy]
            for r in range(K):
                table_ref[slot, m * KK + r * K : m * KK + (r + 1) * K, :] = (
                    ypart[r : r + 1, :] * zpart
                ).astype(BF)

    prepare(0)
    for cyz in range(9):
        if cyz < 8:
            prepare(cyz + 1)
        term = dot(spread_ref[cyz % 2], table_ref[cyz % 2])
        acc_ref[...] = term if cyz == 0 else acc_ref[...] + term


def fine_kernel(
    idx_ref,
    counts_ref,
    arrived_ref,
    fine_ref,
    info_ref,
    xbd_ref,
    yw_ref,
    zw_ref,
    out_ref,
    one_ref,
    coarse_idx_ref,
    pool_ref,
    spread_ref,
    table_ref,
    acc_ref,
    sems,
):
    copies = []
    for level in range(2):
        part = pl.ds(level * 64, 64)
        copies.append(
            pltpu.make_async_copy(
                arrived_ref.at[:, part], pool_ref.at[pl.ds(0, 128), part], sems.at[level]
            )
        )
        copies[-1].start()
    for level in range(2):
        for b in range(SLOT):
            block = fine_ref[level, b]
            pool_ref[128 + b, level * 64 : level * 64 + 16, :] = block[:, 0:128]
            pool_ref[128 + b, level * 64 + 16 : level * 64 + 32, :] = block[:, 128:256]
    pool_ref[144, 0:32, :] = jnp.zeros((32, 128), BF)
    lists = info_ref[...].astype(F32)
    refs, codes, mask = (lists[:, i, :] for i in range(3))
    codes = jnp.where(mask == 1.0, codes, -1.0)
    offset = iota((16, 128), 1).astype(F32)
    place = jnp.full((16, 128), 128.0, F32)
    for j in range(16):
        place = jnp.where(codes[:, j : j + 1] == offset, refs[:, j : j + 1], place)
    coarse_idx_ref[...] = place.astype(jnp.int32) * 32

    blocks = pool_ref.reshape(145 * 128, 128)

    for level in range(2):
        copies[level].wait()
        apply_level(
            level,
            blocks,
            lambda b, code: idx_ref[(level * SLOT + b) * CODES + code],
            xbd_ref,
            yw_ref,
            zw_ref,
            spread_ref,
            table_ref,
            acc_ref,
        )
        for b in range(SLOT):
            rows = jnp.where(b < counts_ref[level, 0], acc_ref[b * K : (b + 1) * K, :], 0.0)
            if level == 0:
                out_ref[0, b] = rows.astype(BF)
            else:
                one_ref[b] = rows


def tail_kernel(
    idx_ref,
    parent_ref,
    code_ref,
    lane_ref,
    summed_ref,
    one_ref,
    xbd_ref,
    yw_ref,
    zw_ref,
    filt_ref,
    fine_in_ref,
    fine_out_ref,
    coarse_out_ref,
    pool_ref,
    spread_ref,
    table_ref,
    acc_ref,
    coarse_ref,
    result_ref,
    sems,
):
    copies = []
    for g in range(8):
        copies.append(
            pltpu.make_async_copy(
                summed_ref.at[:, 1 - g % 2, :, g // 2], pool_ref.at[g], sems.at[g]
            )
        )
        copies[-1].start()
    pool_ref[8, 0, 0:4] = jnp.zeros((4, 8, 128), BF)
    blocks = pool_ref.reshape(9 * 512, 128)
    for copy in copies:
        copy.wait()

    apply_level(
        2,
        blocks,
        lambda b, code: idx_ref[b, code],
        xbd_ref,
        yw_ref,
        zw_ref,
        spread_ref,
        table_ref,
        acc_ref,
    )
    for t in range(SLOT):
        coarse_ref[t] = acc_ref[t * K : (t + 1) * K, :]
    coarse_out_ref[0] = coarse_ref[lane_ref[0]].astype(BF)

    rep_n, tile_n, _, tile_t = factors(filt_ref)
    lane_block = iota((K, KK), 1) // K
    rows = []
    for b in range(SLOT):
        chosen = jnp.where(code_ref[b] // 4 == 1, tile_t[1], tile_t[0])
        rows.append(jnp.where(lane_block == parent_ref[b], chosen, 0.0).astype(BF))
    lowered = dot(jnp.concatenate(rows, axis=0), acc_ref[...].astype(BF)).astype(BF)
    correction = dot(corner_spread(lowered, code_ref), corner_tables(rep_n, tile_n))
    for b in range(SLOT):
        result_ref[b] = (one_ref[b] + correction[b * K : (b + 1) * K, :]).astype(BF)
    copy = pltpu.make_async_copy(result_ref, fine_out_ref.at[1], sems.at[8])
    copy.start()
    copy.wait()


def smem():
    return pl.BlockSpec(memory_space=pltpu.SMEM)


def vmem():
    return pl.BlockSpec(memory_space=pltpu.VMEM)


def anywhere():
    return pl.BlockSpec(memory_space=pl.ANY)


def code_index(codes, mask, places, empty):
    hits = (codes[:, None, :] == jnp.arange(CODES, dtype=jnp.int32)[None, :, None]) & (
        mask[:, None, :] == 1
    )
    return empty + jnp.sum(jnp.where(hits, places[:, None, :] - empty, 0), axis=2)


def body(
    fine_in,
    counts,
    neighbour_refs,
    offset_codes,
    neighbour_mask,
    send_slots,
    parent_of,
    child_code,
    coarse_refs,
    coarse_codes,
    coarse_mask,
    ops_x,
    ops_y,
    ops_z,
    filters,
):
    grp = lax.axis_index("grp").astype(jnp.int32).reshape(1)
    lane = lax.axis_index("lane").astype(jnp.int32).reshape(1)
    send = pl.pallas_call(
        send_kernel,
        in_specs=[smem()] * 4 + [vmem()] * 5,
        out_specs=anywhere(),
        out_shape=jax.ShapeDtypeStruct((128, 136, 128), BF),
        scratch_shapes=[
            pltpu.VMEM((128, 128, 128), BF),
            pltpu.VMEM((128, 8, 128), BF),
            pltpu.VMEM((SLOT + 1, K, KK), F32),
            pltpu.SemaphoreType.DMA((5,)),
        ],
        name="send",
    )(
        parent_of,
        child_code,
        send_slots,
        grp,
        fine_in,
        filters,
        coarse_refs,
        coarse_codes,
        coarse_mask,
    )
    arrived = lax.all_to_all(send, AXES, split_axis=0, concat_axis=0, tiled=True)

    summed, info = pl.pallas_call(
        place_kernel,
        in_specs=[smem(), anywhere()],
        out_specs=[vmem(), vmem()],
        out_shape=[
            jax.ShapeDtypeStruct((128, 32, 128), BF),
            jax.ShapeDtypeStruct((16, 8, 128), BF),
        ],
        scratch_shapes=[pltpu.VMEM((4, 2, 16, 8, 128), BF), pltpu.SemaphoreType.DMA],
        name="place",
    )(grp, arrived.reshape(4, 2, 16, 136, 128))
    summed = lax.all_to_all(summed, AXES, split_axis=0, concat_axis=0, tiled=True)

    repeat, tiled = spreads()
    yw = jnp.einsum("lmcpr,pk->lmcrk", ops_y, repeat, preferred_element_type=F32)
    zw = jnp.einsum("lmcqs,qk->lmcsk", ops_z, tiled, preferred_element_type=F32)
    yw = yw.reshape(3, 12, K, KK)
    zw = zw.reshape(3, 12, K, KK)
    xm = jnp.transpose(ops_x, (0, 1, 3, 2, 4)).reshape(3, 64, 48)
    row, col = iota((256, 64), 0), iota((256, 64), 1)
    grow = ((row // 64 == col // 16) & (row % 16 == col % 16)).astype(BF)
    row, col = iota((48, 192), 0), iota((48, 192), 1)
    wide = (col % 48 == row).astype(BF)
    row, col = iota((256, 192), 0), iota((256, 192), 1)
    own = (row // 16) % 4 == col // 48
    xbd = jnp.einsum("ij,ljk->lik", grow, xm)
    xbd = jnp.einsum("lik,kn->lin", xbd, wide)
    xbd = jnp.where(own[None], xbd, jnp.zeros_like(xbd))

    empty = 144 * 128
    tables = []
    for level in range(2):
        refs = neighbour_refs[level]
        far = refs - SLOT
        places = jnp.where(
            refs < SLOT,
            (128 + refs) * 128 + level * 64,
            (far // CAP) * 128 + level * 64 + (far % CAP) * 32,
        )
        tables.append(code_index(offset_codes[level], neighbour_mask[level], places, empty))
    idx = jnp.concatenate([t.reshape(-1) for t in tables])
    work = [
        pltpu.VMEM((2, KK, TERMS * KK), BF),
        pltpu.VMEM((2, TERMS * KK, KK), BF),
        pltpu.VMEM((KK, KK), F32),
    ]
    fine_out, one, coarse_idx = pl.pallas_call(
        fine_kernel,
        in_specs=[smem()] * 2 + [anywhere()] + [vmem()] * 5,
        out_specs=[pl.BlockSpec((1, SLOT, K, KK), lambda i: (0, 0, 0, 0)), vmem(), vmem()],
        out_shape=[
            jax.ShapeDtypeStruct((2, SLOT, K, KK), BF),
            jax.ShapeDtypeStruct((SLOT, K, KK), F32),
            jax.ShapeDtypeStruct((16, 128), jnp.int32),
        ],
        grid=(1,),
        scratch_shapes=[pltpu.VMEM((145, 128, 128), BF)]
        + work
        + [pltpu.SemaphoreType.DMA((2,))],
        name="fine",
        cost_estimate=pl.CostEstimate(
            flops=10_000_000_000, bytes_accessed=6_000_000, transcendentals=0
        ),
    )(idx, counts, arrived, fine_in, info, xbd, yw, zw)

    fine_out, coarse_out = pl.pallas_call(
        tail_kernel,
        in_specs=[smem()] * 4 + [anywhere()] + [vmem()] * 5 + [anywhere()],
        out_specs=[anywhere(), vmem()],
        out_shape=[
            jax.ShapeDtypeStruct((2, SLOT, K, KK), BF),
            jax.ShapeDtypeStruct((1, K, KK), BF),
        ],
        scratch_shapes=[pltpu.VMEM((9, 4, 16, 8, 128), BF)]
        + work
        + [
            pltpu.VMEM((SLOT, K, KK), F32),
            pltpu.VMEM((SLOT, K, KK), BF),
            pltpu.SemaphoreType.DMA((9,)),
        ],
        input_output_aliases={10: 0},
        name="tail",
    )(
        coarse_idx,
        parent_of,
        child_code,
        lane,
        summed.reshape(4, 2, 16, 4, 8, 128),
        one,
        xbd,
        yw,
        zw,
        filters,
        fine_out,
    )
    return fine_out, coarse_out


def solution(mesh):
    blocks = P(None, AXES, None, None)
    table = P(None, AXES, None)
    in_specs = (
        blocks,
        P(None, AXES),
        table,
        table,
        table,
        table,
        P(AXES),
        P(AXES),
        P(AXES, None),
        P(AXES, None),
        P(AXES, None),
        P(),
        P(),
        P(),
        P(),
    )
    out_specs = (blocks, P(AXES, None, None))
    return jax.shard_map(body, mesh=mesh, in_specs=in_specs, out_specs=out_specs, check_vma=False)
```

time: 124 us -> 106 us (0.85)
  Pallas kernels: 35.2 us -> 23 us
  other arithmetic: 4.8 us -> 1.26 us
    pallas_call x4, Pallas kernels: 35.2 us -> 23 us  [the longest x1 9.59 us: body(): pl.pallas_call(fine_kernel, in_specs=[smem()] * 2 + [anywhere()] + [vmem(...]
    all_to_all x1, waiting for transfers between devices: 56.3 us -> 49.5 us  [body(): lax.all_to_all(send, AXES, split_axis=0, concat_axis=0, tiled=True)]
    all_to_all x1, waiting for transfers between devices: 2.14 us -> 8.38 us  [body(): lax.all_to_all(summed, AXES, split_axis=0, concat_axis=0, tiled=True)]
    all_to_all x1, starting transfers between devices: 8.45 us -> 4.56 us  [body(): lax.all_to_all(summed, AXES, split_axis=0, concat_axis=0, tiled=True)]
    all_to_all x1, starting transfers between devices: 8.54 us -> 11.9 us  [body(): lax.all_to_all(send, AXES, split_axis=0, concat_axis=0, tiled=True)]
    another operation x3 -> x0, other arithmetic: 1.97 us -> none
  transfers between devices with their start and end apart: 2 -> 2, of which waited for: 2 -> 2; matrix products, arithmetic and copies ran while one was open for 6% -> 6% of each run, Pallas kernels for 4% -> 9%
where the time goes in v2:
time: 106 us; the launch traced here: 105 us
  waiting for transfers between devices  57.9 us (55%)
  Pallas kernels  23 us (22%)
  starting transfers between devices  16.5 us (16%)
  matrix products  3.54 us (3%)
  local copies, waits for them, and re-layouts  2.15 us (2%)
  other arithmetic  1.26 us (1%)
  between operations  1.07 us (1%)
    all_to_all x1, waiting for transfers between devices, body(): lax.all_to_all(send, AXES, split_axis=0, concat_axis=0, tiled=True)  49.5 us
    all_to_all x1, starting transfers between devices, body(): lax.all_to_all(send, AXES, split_axis=0, concat_axis=0, tiled=True)  11.9 us
    pallas_call x1, Pallas kernels, body(): pl.pallas_call(fine_kernel, in_specs=[smem()] * 2 + [anywhere()] + [vmem(...  9.59 us
    all_to_all x1, waiting for transfers between devices, body(): lax.all_to_all(summed, AXES, split_axis=0, concat_axis=0, tiled=True)  8.38 us
    pallas_call x1, Pallas kernels, body(): pl.pallas_call(tail_kernel, in_specs=[smem()] * 4 + [anywhere()] + [vmem(...  7.48 us
    all_to_all x1, starting transfers between devices, body(): lax.all_to_all(summed, AXES, split_axis=0, concat_axis=0, tiled=True)  4.56 us
    pallas_call x1, Pallas kernels, body(): pl.pallas_call(send_kernel, in_specs=[smem()] * 4 + [vmem()] * 5, out_spe...  3.84 us
  transfers between devices with their start and end apart: 2, of which 2 were waited for; matrix products, arithmetic and copies ran while one was open for 6% of the time, Pallas kernels for 9%

profile of v2, /device:TPU:1, one launch (start us, length us, event | category | flops | bytes accessed | tf_op | source)
XLA Modules:
  0.0 105.4 jit_solution(17915376365785727471)
XLA Ops:
  0.6 0.0 copy-start
  0.7 3.8 %send.1 = bf16[128,136,128]{2,1,0:T(8,128)(2,1)} custom-call(s32[16]{0:T(128)} %parent_ref.3, s32[16]{0:T(128)} %code_ref.3, s32[2,1,256]{2,1,0:T(1,128)} %slots_ref.1, s32[1]{0:T(128)} %bitcast.10.grp_ref, bf16[2,16,16,256]{3,2,1,0:T(8,128)(2,1)} %fine_ref.3, bf16[2,16,16]{2,1,0:T(8,128)(2,1)} %filt_ref.3, s32[1,16]{1,0:T(1,128)} %refs_ref.1, ...), custom_call_target="tpu_custom_call" | custom-call | tf_op jit(solution)/shard_map/send/pallas_call | solution.py:355
  4.5 0.0 copy-start.4
  4.5 0.0 copy-start.5
  4.5 0.0 copy-start.6
  4.5 0.0 copy-start.7
  4.5 0.0 copy-start.3
  4.6 0.0 copy-start.2
  4.6 11.9 %all-to-all-start = ((bf16[128,136,128]{2,1,0:T(8,128)(2,1)}), bf16[128,136,128]{2,1,0:T(8,128)(2,1)}, u32[]{:S(2)}, u32[]{:S(2)}) async-start(bf16[128,136,128]{2,1,0:T(8,128)(2,1)} %send.1), calls=%async_computation | async-start | bytes 8912896 | tf_op jit(solution)/shard_map/all_to_all | solution.py:378
  16.5 0.0 copy-done.4
  16.5 0.0 copy-done.5
  16.5 0.0 copy-done.6
  16.6 0.3 select_reduce_fusion
  16.9 0.1 add.171
  17.0 0.1 add.163
  17.1 0.0 copy-done.7
  17.1 0.7 copy.31.counts_ref
  17.7 0.0 copy-done.3
  17.7 0.1 copy.27
  17.9 0.1 reshape.256
  18.2 0.2 fusion
  18.4 0.3 fusion.5
  18.6 1.1 %convolution_select_fusion.xbd_ref = bf16[3,256,192]{2,1,0:T(8,128)(2,1)} fusion(bf16[3,256,48]{1,2,0:T(8,128)(2,1)S(1)} %bitcast.99, pred[256,192]{1,0:T(8,128)(4,1)S(1)} %fusion, s32[192]{0:T(256)S(1)} %get-tuple-element.36, s32[192]{0:T(256)S(1)} %get-tuple-element.37, pred[192]{0:T(512)(128)(4,1)S(1)} %compare_and_fusion), kind=kOutput, calls=%fused_computation | convolution fusion | flops 14321664 | bytes 419520 | tf_op jit(solution)/shard_map/lik,kn->lin/dot_general | solution.py:406
  19.7 0.0 copy-done
  19.7 1.1 %fusion.25 = f32[256,3,4,3,16]{0,4,3,2,1:T(8,128)} fusion(bf16[3,4,3,16,16]{4,3,2,1,0:T(8,128)(2,1)S(1)} %copy-done, s32[256]{0:T(256)S(1)} %get-tuple-element.34, s32[256]{0:T(256)S(1)} %get-tuple-element.35, pred[256]{0:T(512)(128)(4,1)S(1)} %fusion.60), kind=kOutput, calls=%fused_computation.38 | convolution fusion | flops 4726784 | bytes 610560 | tf_op jit(solution)/shard_map/lmcpr,pk->lmcrk/dot_general | solution.py:394
  20.8 0.0 copy-done.2
  20.8 1.1 %fusion.28 = f32[256,3,4,3,16]{0,4,3,2,1:T(8,128)} fusion(bf16[3,4,3,16,16]{4,3,2,1,0:T(8,128)(2,1)S(1)} %copy-done.2, s32[256]{0:T(256)S(1)} %get-tuple-element.20, s32[256]{0:T(256)S(1)} %get-tuple-element.28, pred[256]{0:T(512)(128)(4,1)S(1)} %get-tuple-element.24), kind=kOutput, calls=%fused_computation.40 | convolution fusion | flops 4726784 | bytes 610560 | tf_op jit(solution)/shard_map/lmcqs,qk->lmcsk/dot_general | solution.py:395
  21.9 49.5 %all-to-all-done.arrived_ref = bf16[128,136,128]{2,1,0:T(8,128)(2,1)} async-done(((bf16[128,136,128]{2,1,0:T(8,128)(2,1)}), bf16[128,136,128]{2,1,0:T(8,128)(2,1)}, u32[]{:S(2)}, u32[]{:S(2)}) %all-to-all-start) | async-done | bytes 4456480 | tf_op jit(solution)/shard_map/all_to_all | solution.py:378
  71.4 2.1 %place.1 = (bf16[128,32,128]{2,1,0:T(8,128)(2,1)}, bf16[16,8,128]{2,1,0:T(8,128)(2,1)}) custom-call(s32[1]{0:T(128)} %bitcast.10.grp_ref, bf16[4,2,16,136,128]{4,3,2,1,0:T(8,128)(2,1)} %bitcast.11.arrived_ref), custom_call_target="tpu_custom_call" | custom-call | tf_op jit(solution)/shard_map/place/pallas_call | solution.py:380
  73.5 4.6 %all-to-all-start.1 = ((bf16[128,32,128]{2,1,0:T(8,128)(2,1)}), bf16[128,32,128]{2,1,0:T(8,128)(2,1)S(1)}, u32[]{:S(2)}, u32[]{:S(2)}) async-start(bf16[128,32,128]{2,1,0:T(8,128)(2,1)} %get-tuple-element.9), calls=%async_computation.1 | async-start | bytes 2097152 | tf_op jit(solution)/shard_map/all_to_all | solution.py:391
  78.1 0.7 pad_add_fusion.idx_ref
  78.8 9.6 %fine.1 = (bf16[2,16,16,256]{3,2,1,0:T(8,128)(2,1)}, f32[16,16,256]{2,1,0:T(8,128)}, s32[16,128]{1,0:T(8,128)}) custom-call(s32[864]{0:T(1024)} %pad_add_fusion.idx_ref, s32[2,1]{1,0:T(2,128)} %copy.31.counts_ref, bf16[128,136,128]{2,1,0:T(8,128)(2,1)} %all-to-all-done.arrived_ref, bf16[2,16,16,256]{3,2,1,0:T(8,128)(2,1)} %fine_ref.3, ...), custom_call_target="tpu_custom_call" | custom-call | flops 10000000000 | bytes 6000000 | tf_op jit(solution)/shard_map/fine/pallas_call | solution.py:426
  88.4 8.4 %all-to-all-done.1 = bf16[128,32,128]{2,1,0:T(8,128)(2,1)S(1)} async-done(((bf16[128,32,128]{2,1,0:T(8,128)(2,1)}), bf16[128,32,128]{2,1,0:T(8,128)(2,1)S(1)}, u32[]{:S(2)}, u32[]{:S(2)}) %all-to-all-start.1) | async-done | bytes 1048608 | tf_op jit(solution)/shard_map/all_to_all | solution.py:391
  96.7 0.0 copy-start.1
  96.7 1.0 copy-done.1
  97.7 7.5 %tail.1 = (bf16[2,16,16,256]{3,2,1,0:T(8,128)(2,1)}, bf16[1,16,256]{2,1,0:T(8,128)(2,1)}) custom-call(s32[16,128]{1,0:T(8,128)} %get-tuple-element.8.idx_ref, s32[16]{0:T(128)} %parent_ref.3, s32[16]{0:T(128)} %code_ref.3, s32[1]{0:T(128)} %bitcast.26.lane_ref, bf16[4,2,16,4,8,128]{5,4,3,2,1,0:T(8,128)(2,1)} %bitcast.92, ...), custom_call_target="tpu_custom_call", output_to_operand_aliasing={{0}: (10, {})} | custom-call | tf_op jit(solution)/shard_map/tail/pallas_call | solution.py:445
  (17 shorter events, 0.1 us)
Async XLA Ops:
  0.6 19.1 %copy-start = (bf16[3,4,3,16,16]{4,3,2,1,0:T(8,128)(2,1)S(1)}, bf16[3,4,3,16,16]{4,3,2,1,0:T(8,128)(2,1)}, u32[]{:S(2)}) copy-start(bf16[3,4,3,16,16]{4,3,2,1,0:T(8,128)(2,1)} %param.27) | copy-start | bytes 55300
  4.5 12.0 %copy-start.4 = (s32[2,16,16]{2,1,0:T(8,128)S(1)}, s32[2,16,16]{2,1,0:T(8,128)}, u32[]{:S(2)}) copy-start(s32[2,16,16]{2,1,0:T(8,128)} %param.19) | copy-start | bytes 6148
  4.5 12.0 %copy-start.5 = (s32[2,16,16]{2,1,0:T(8,128)S(1)}, s32[2,16,16]{2,1,0:T(8,128)}, u32[]{:S(2)}) copy-start(s32[2,16,16]{2,1,0:T(8,128)} %param.17) | copy-start | bytes 6148
  4.5 12.0 %copy-start.6 = (s32[2,16,16]{2,1,0:T(8,128)S(1)}, s32[2,16,16]{2,1,0:T(8,128)}, u32[]{:S(2)}) copy-start(s32[2,16,16]{2,1,0:T(8,128)} %param.18) | copy-start | bytes 6148
  4.5 12.5 %copy-start.7 = (s32[2,1]{0,1:T(1,128)S(1)}, s32[2,1]{0,1:T(1,128)}, u32[]{:S(2)}) copy-start(s32[2,1]{0,1:T(1,128)} %param.16) | copy-start | bytes 28
  4.5 13.2 %copy-start.3 = (bf16[3,4,3,16,16]{4,3,2,1,0:T(8,128)(2,1)S(1)}, bf16[3,4,3,16,16]{4,3,2,1,0:T(8,128)(2,1)}, u32[]{:S(2)}) copy-start(bf16[3,4,3,16,16]{4,3,2,1,0:T(8,128)(2,1)} %param.26) | copy-start | bytes 55300
  4.6 16.3 %copy-start.2 = (bf16[3,4,3,16,16]{4,3,2,1,0:T(8,128)(2,1)S(1)}, bf16[3,4,3,16,16]{4,3,2,1,0:T(8,128)(2,1)}, u32[]{:S(2)}) copy-start(bf16[3,4,3,16,16]{4,3,2,1,0:T(8,128)(2,1)} %param.28) | copy-start | bytes 55300
  4.6 66.9 %all-to-all-start = ((bf16[128,136,128]{2,1,0:T(8,128)(2,1)}), bf16[128,136,128]{2,1,0:T(8,128)(2,1)}, u32[]{:S(2)}, u32[]{:S(2)}) async-start(bf16[128,136,128]{2,1,0:T(8,128)(2,1)} %send.1), calls=%async_computation | async-start | bytes 8912896 | tf_op jit(solution)/shard_map/all_to_all | solution.py:378
  73.5 23.2 %all-to-all-start.1 = ((bf16[128,32,128]{2,1,0:T(8,128)(2,1)}), bf16[128,32,128]{2,1,0:T(8,128)(2,1)S(1)}, u32[]{:S(2)}, u32[]{:S(2)}) async-start(bf16[128,32,128]{2,1,0:T(8,128)(2,1)} %get-tuple-element.9), calls=%async_computation.1 | async-start | bytes 2097152 | tf_op jit(solution)/shard_map/all_to_all | solution.py:391
  96.7 1.0 copy-start.1

commit v3 on v2

--- a/solution.py
+++ b/solution.py
@@ -11,6 +11,7 @@
 SLOT = 16
 CAP = 2
 CODES = 27
+GROUP = 4
 BF = jnp.bfloat16
 F32 = jnp.float32
 AXES = ("grp", "lane")
@@ -64,7 +65,6 @@
     parent_ref,
     code_ref,
     slots_ref,
-    grp_ref,
     fine_ref,
     filt_ref,
     refs_ref,
@@ -77,7 +77,8 @@
     sems,
 ):
     copies = []
-    for chunk in range(4):
+    for chunk in range(8):
+
         def fill(r, carry):
             for level in range(2):
                 for c in range(CAP):
@@ -88,8 +89,8 @@
                     pack_ref[r, at + 16 : at + 32, :] = block[:, 128:256]
             return carry
 
-        lax.fori_loop(chunk * 32, chunk * 32 + 32, fill, 0, unroll=4)
-        here = pl.ds(chunk * 32, 32)
+        lax.fori_loop(chunk * 16, chunk * 16 + 16, fill, 0, unroll=4)
+        here = pl.ds(chunk * 16, 16)
         copies.append(
             pltpu.make_async_copy(
                 pack_ref.at[here], send_ref.at[here, pl.ds(0, 128)], sems.at[chunk]
@@ -105,7 +106,7 @@
         rows.append(jnp.where(lane_block == b, chosen, 0.0).astype(BF))
     lifted = dot(jnp.concatenate(rows, axis=0), fine_ref[1].reshape(SLOT * K, KK)).astype(BF)
     moved = dot(corner_spread(lifted, code_ref), corner_tables(rep_t, tile_t))
-    parity = grp_ref[0] % 2
+    parity = lax.axis_index("grp") % 2
     info = jnp.concatenate([refs_ref[...], codes_ref[...]] + [mask_ref[...]] * 6, axis=0)
     wide = (iota((16, 128), 0) == iota((16, 128), 1)).astype(BF)
     info = dot(info.astype(F32).astype(BF), wide).astype(BF)
@@ -122,17 +123,18 @@
             for top in range(2):
                 tile = acc_ref[t, top * 8 : top * 8 + 8, half * 128 : half * 128 + 128].astype(BF)
                 j = t * 4 + half * 2 + top
-                piece_ref[(2 * (j // 16) + 1 - parity) * 16 + j % 16] = tile
+                piece_ref[(2 * (j % 4) + 1 - parity) * 16 + j // 4] = tile
     copies.append(
-        pltpu.make_async_copy(piece_ref, send_ref.at[:, pl.ds(128, 8)], sems.at[4])
+        pltpu.make_async_copy(piece_ref, send_ref.at[:, pl.ds(128, 8)], sems.at[8])
     )
     copies[-1].start()
     for copy in copies:
         copy.wait()
 
 
-def place_kernel(grp_ref, arrived_ref, out_ref, info_ref, piece_ref, sem):
-    parity = grp_ref[0] % 2
+def place_kernel(arrived_ref, out_ref, info_ref, piece_ref, sem):
+    grp = lax.axis_index("grp")
+    parity = grp % 2
     copy = pltpu.make_async_copy(arrived_ref.at[:, :, :, pl.ds(128, 8)], piece_ref, sem)
     copy.start()
     copy.wait()
@@ -145,7 +147,7 @@
     mine = jnp.concatenate(sums, axis=0).astype(BF)
     for r in range(128):
         out_ref[r] = mine
-    info_ref[...] = piece_ref[grp_ref[0] // 2, parity]
+    info_ref[...] = piece_ref[grp // 2, parity]
 
 
 def apply_level(level, blocks, place, xbd_ref, yw_ref, zw_ref, spread_ref, table_ref, acc_ref):
@@ -153,11 +155,11 @@
 
     def prepare(cyz):
         cy, cz, slot = cyz // 3, cyz % 3, cyz % 2
-        for g4 in range(4):
+        for group in range(SLOT // GROUP):
             parts = []
-            for b4 in range(4):
+            for b in range(group * GROUP, (group + 1) * GROUP):
                 for cx in range(3):
-                    at = pl.multiple_of(place(g4 * 4 + b4, 9 * cx + cyz), 32)
+                    at = pl.multiple_of(place(b, 9 * cx + cyz), 32)
                     parts.append(
                         jnp.concatenate(
                             [blocks[pl.ds(at, 16), :], blocks[pl.ds(at + 16, 16), :]], axis=1
@@ -165,9 +167,10 @@
                     )
             spread = dot(xbd, jnp.concatenate(parts, axis=0)).astype(BF)
             for m in range(TERMS):
-                spread_ref[slot, g4 * 64 : (g4 + 1) * 64, m * KK : (m + 1) * KK] = spread[
-                    m * 64 : (m + 1) * 64, :
-                ]
+                size = GROUP * K
+                spread_ref[slot, group * size : (group + 1) * size, m * KK : (m + 1) * KK] = (
+                    spread[m * size : (m + 1) * size, :]
+                )
         for m in range(TERMS):
             zpart = zw_ref[level, m * 3 + cz]
             ypart = yw_ref[level, m * 3 + cy]
@@ -253,7 +256,6 @@
     idx_ref,
     parent_ref,
     code_ref,
-    lane_ref,
     summed_ref,
     one_ref,
     xbd_ref,
@@ -275,11 +277,11 @@
     for g in range(8):
         copies.append(
             pltpu.make_async_copy(
-                summed_ref.at[:, 1 - g % 2, :, g // 2], pool_ref.at[g], sems.at[g]
+                summed_ref.at[:, 1 - g % 2, g // 2], pool_ref.at[g], sems.at[g]
             )
         )
         copies[-1].start()
-    pool_ref[8, 0, 0:4] = jnp.zeros((4, 8, 128), BF)
+    pool_ref[8, 0:4] = jnp.zeros((4, 8, 128), BF)
     blocks = pool_ref.reshape(9 * 512, 128)
     for copy in copies:
         copy.wait()
@@ -297,7 +299,7 @@
     )
     for t in range(SLOT):
         coarse_ref[t] = acc_ref[t * K : (t + 1) * K, :]
-    coarse_out_ref[0] = coarse_ref[lane_ref[0]].astype(BF)
+    coarse_out_ref[0] = coarse_ref[lax.axis_index("lane")].astype(BF)
 
     rep_n, tile_n, _, tile_t = factors(filt_ref)
     lane_block = iota((K, KK), 1) // K
@@ -320,6 +322,10 @@
 
 def vmem():
     return pl.BlockSpec(memory_space=pltpu.VMEM)
+
+
+def room(mib):
+    return pltpu.CompilerParams(vmem_limit_bytes=mib * 1024 * 1024)
 
 
 def anywhere():
@@ -350,25 +356,22 @@
     ops_z,
     filters,
 ):
-    grp = lax.axis_index("grp").astype(jnp.int32).reshape(1)
-    lane = lax.axis_index("lane").astype(jnp.int32).reshape(1)
     send = pl.pallas_call(
         send_kernel,
-        in_specs=[smem()] * 4 + [vmem()] * 5,
+        in_specs=[smem()] * 3 + [vmem()] * 5,
         out_specs=anywhere(),
         out_shape=jax.ShapeDtypeStruct((128, 136, 128), BF),
         scratch_shapes=[
             pltpu.VMEM((128, 128, 128), BF),
             pltpu.VMEM((128, 8, 128), BF),
             pltpu.VMEM((SLOT + 1, K, KK), F32),
-            pltpu.SemaphoreType.DMA((5,)),
+            pltpu.SemaphoreType.DMA((9,)),
         ],
         name="send",
     )(
         parent_of,
         child_code,
         send_slots,
-        grp,
         fine_in,
         filters,
         coarse_refs,
@@ -379,16 +382,17 @@
 
     summed, info = pl.pallas_call(
         place_kernel,
-        in_specs=[smem(), anywhere()],
+        in_specs=[anywhere()],
         out_specs=[vmem(), vmem()],
         out_shape=[
             jax.ShapeDtypeStruct((128, 32, 128), BF),
             jax.ShapeDtypeStruct((16, 8, 128), BF),
         ],
         scratch_shapes=[pltpu.VMEM((4, 2, 16, 8, 128), BF), pltpu.SemaphoreType.DMA],
+        compiler_params=room(8),
         name="place",
-    )(grp, arrived.reshape(4, 2, 16, 136, 128))
-    summed = lax.all_to_all(summed, AXES, split_axis=0, concat_axis=0, tiled=True)
+    )(arrived.reshape(4, 2, 16, 136, 128))
+    summed = lax.all_to_all(summed, AXES[::-1], split_axis=0, concat_axis=0, tiled=True)
 
     repeat, tiled = spreads()
     yw = jnp.einsum("lmcpr,pk->lmcrk", ops_y, repeat, preferred_element_type=F32)
@@ -396,12 +400,13 @@
     yw = yw.reshape(3, 12, K, KK)
     zw = zw.reshape(3, 12, K, KK)
     xm = jnp.transpose(ops_x, (0, 1, 3, 2, 4)).reshape(3, 64, 48)
-    row, col = iota((256, 64), 0), iota((256, 64), 1)
-    grow = ((row // 64 == col // 16) & (row % 16 == col % 16)).astype(BF)
-    row, col = iota((48, 192), 0), iota((48, 192), 1)
+    size = GROUP * K
+    row, col = iota((4 * size, 64), 0), iota((4 * size, 64), 1)
+    grow = ((row // size == col // K) & (row % K == col % K)).astype(BF)
+    row, col = iota((48, 3 * size), 0), iota((48, 3 * size), 1)
     wide = (col % 48 == row).astype(BF)
-    row, col = iota((256, 192), 0), iota((256, 192), 1)
-    own = (row // 16) % 4 == col // 48
+    row, col = iota((4 * size, 3 * size), 0), iota((4 * size, 3 * size), 1)
+    own = (row % size) // K == col // 48
     xbd = jnp.einsum("ij,ljk->lik", grow, xm)
     xbd = jnp.einsum("lik,kn->lin", xbd, wide)
     xbd = jnp.where(own[None], xbd, jnp.zeros_like(xbd))
@@ -436,6 +441,7 @@
         scratch_shapes=[pltpu.VMEM((145, 128, 128), BF)]
         + work
         + [pltpu.SemaphoreType.DMA((2,))],
+        compiler_params=room(20),
         name="fine",
         cost_estimate=pl.CostEstimate(
             flops=10_000_000_000, bytes_accessed=6_000_000, transcendentals=0
@@ -444,27 +450,27 @@
 
     fine_out, coarse_out = pl.pallas_call(
         tail_kernel,
-        in_specs=[smem()] * 4 + [anywhere()] + [vmem()] * 5 + [anywhere()],
+        in_specs=[smem()] * 3 + [anywhere()] + [vmem()] * 5 + [anywhere()],
         out_specs=[anywhere(), vmem()],
         out_shape=[
             jax.ShapeDtypeStruct((2, SLOT, K, KK), BF),
             jax.ShapeDtypeStruct((1, K, KK), BF),
         ],
-        scratch_shapes=[pltpu.VMEM((9, 4, 16, 8, 128), BF)]
+        scratch_shapes=[pltpu.VMEM((9, 64, 8, 128), BF)]
         + work
         + [
             pltpu.VMEM((SLOT, K, KK), F32),
             pltpu.VMEM((SLOT, K, KK), BF),
             pltpu.SemaphoreType.DMA((9,)),
         ],
-        input_output_aliases={10: 0},
+        input_output_aliases={9: 0},
+        compiler_params=room(16),
         name="tail",
     )(
         coarse_idx,
         parent_of,
         child_code,
-        lane,
-        summed.reshape(4, 2, 16, 4, 8, 128),
+        summed.reshape(64, 2, 4, 8, 128),
         one,
         xbd,
         yw,

time: 106 us -> 103 us (0.972)
  waiting for transfers between devices: 57.9 us -> 62.7 us
  Pallas kernels: 23 us -> 20.2 us
  matrix products: 3.54 us -> 1.11 us
  local copies, waits for them, and re-layouts: 2.15 us -> 0.6 us
    all_to_all x1, waiting for transfers between devices: 49.5 us -> 52.5 us  [body(): lax.all_to_all(send, AXES, split_axis=0, concat_axis=0, tiled=True)]
    all_to_all x1, waiting for transfers between devices: 8.38 us -> 10.3 us  [body(): lax.all_to_all(summed, AXES[::-1], split_axis=0, concat_axis=0, tiled=True)]
    pallas_call x3, Pallas kernels: 13.4 us -> 11.6 us  [the longest x1 5.79 us: body(): pl.pallas_call(tail_kernel, in_specs=[smem()] * 3 + [anywhere()] + [vmem(...]
    unnamed x17 -> x23, local copies, waits for them, and re-layouts: 1.71 us -> 0.16 us
  transfers between devices with their start and end apart: 2 -> 2, of which waited for: 2 -> 2; matrix products, arithmetic and copies ran while one was open for 6% -> 2% of each run, Pallas kernels for 9% -> 8%
where the time goes in v3:
time: 103 us
  waiting for transfers between devices  62.7 us (61%)
  Pallas kernels  20.2 us (20%)
  starting transfers between devices  16.5 us (16%)
  between operations  1.13 us (1%)
  matrix products  1.11 us (1%)
    all_to_all x1, waiting for transfers between devices, body(): lax.all_to_all(send, AXES, split_axis=0, concat_axis=0, tiled=True)  52.5 us
    all_to_all x1, starting transfers between devices, body(): lax.all_to_all(send, AXES, split_axis=0, concat_axis=0, tiled=True)  11.9 us
    all_to_all x1, waiting for transfers between devices, body(): lax.all_to_all(summed, AXES[::-1], split_axis=0, concat_axis=0, tiled=True)  10.3 us
    pallas_call x1, Pallas kernels, body(): pl.pallas_call(fine_kernel, in_specs=[smem()] * 2 + [anywhere()] + [vmem(...  8.64 us
    pallas_call x1, Pallas kernels, body(): pl.pallas_call(tail_kernel, in_specs=[smem()] * 3 + [anywhere()] + [vmem(...  5.79 us
    all_to_all x1, starting transfers between devices, body(): lax.all_to_all(summed, AXES[::-1], split_axis=0, concat_axis=0, tiled=True)  4.56 us
    pallas_call x1, Pallas kernels, body(): pl.pallas_call(send_kernel, in_specs=[smem()] * 3 + [vmem()] * 5, out_spe...  3.72 us
  transfers between devices with their start and end apart: 2, of which 2 were waited for; matrix products, arithmetic and copies ran while one was open for 2% of the time, Pallas kernels for 8%

profile of v3, /device:TPU:1, one launch (start us, length us, event | category | flops | bytes accessed | tf_op | source)
XLA Modules:
  0.0 102.9 jit_solution(12450486253835963243)
XLA Ops:
  0.6 0.0 copy-start
  0.6 3.7 %send.1 = bf16[128,136,128]{2,1,0:T(8,128)(2,1)} custom-call(s32[16]{0:T(128)} %parent_ref.3, s32[16]{0:T(128)} %code_ref.3, s32[2,1,256]{2,1,0:T(1,128)} %slots_ref.1, bf16[2,16,16,256]{3,2,1,0:T(8,128)(2,1)} %fine_ref.3, bf16[2,16,16]{2,1,0:T(8,128)(2,1)} %filt_ref.3, s32[1,16]{1,0:T(1,128)} %refs_ref.1, s32[1,16]{1,0:T(1,128)} %codes_ref.1, s32[1,16]{1,0:T(1,128)} %mask_ref.1), custom_call_target="tpu_custom_call" | custom-call | tf_op jit(solution)/shard_map/send/pallas_call | solution.py:359
  4.4 0.0 copy-start.7
  4.4 0.0 copy-start.8
  4.4 0.0 copy-start.9
  4.4 0.0 copy-start.10
  4.4 0.0 copy-start.6
  4.4 0.0 copy-start.5
  4.4 11.9 %all-to-all-start = ((bf16[128,136,128]{2,1,0:T(8,128)(2,1)}), bf16[128,136,128]{2,1,0:T(8,128)(2,1)}, u32[]{:S(2)}, u32[]{:S(2)}) async-start(bf16[128,136,128]{2,1,0:T(8,128)(2,1)} %send.1), calls=%async_computation | async-start | bytes 8912896 | tf_op jit(solution)/shard_map/all_to_all | solution.py:381
  16.3 0.0 copy-done.7
  16.4 0.0 copy-done.8
  16.4 0.0 copy-done.9
  16.4 0.3 select_reduce_fusion
  16.7 0.1 add.171
  16.8 0.1 add.163
  16.9 0.0 copy-done.10
  16.9 0.1 copy.31.counts_ref
  17.0 0.0 copy-done.6
  17.0 0.1 copy.27
  17.2 0.1 reshape.253
  17.5 0.2 fusion.1
  17.7 0.3 fusion.9
  18.0 0.0 copy-start.1
  18.0 0.3 convolution_select_fusion.xbd_ref
  18.3 0.0 copy-done
  18.3 0.3 fusion.32
  18.6 0.0 copy-done.5
  18.6 0.3 fusion.29
  18.9 52.5 %all-to-all-done.arrived_ref = bf16[128,136,128]{2,1,0:T(8,128)(2,1)} async-done(((bf16[128,136,128]{2,1,0:T(8,128)(2,1)}), bf16[128,136,128]{2,1,0:T(8,128)(2,1)}, u32[]{:S(2)}, u32[]{:S(2)}) %all-to-all-start) | async-done | bytes 4456480 | tf_op jit(solution)/shard_map/all_to_all | solution.py:381
  71.3 2.1 %place.1 = (bf16[128,32,128]{2,1,0:T(8,128)(2,1)}, bf16[16,8,128]{2,1,0:T(8,128)(2,1)S(1)}) custom-call(bf16[4,2,16,136,128]{4,3,2,1,0:T(8,128)(2,1)} %bitcast.10.arrived_ref), custom_call_target="tpu_custom_call" | custom-call | tf_op jit(solution)/shard_map/place/pallas_call | solution.py:383
  73.4 4.6 %all-to-all-start.1 = ((bf16[128,32,128]{2,1,0:T(8,128)(2,1)}), bf16[128,32,128]{2,1,0:T(8,128)(2,1)S(1)}, u32[]{:S(2)}, u32[]{:S(2)}) async-start(bf16[128,32,128]{2,1,0:T(8,128)(2,1)} %get-tuple-element.9), calls=%async_computation.1 | async-start | bytes 2097152 | tf_op jit(solution)/shard_map/all_to_all | solution.py:395
  78.0 0.1 pad_add_fusion.idx_ref
  78.0 0.0 copy-done.1
  78.0 0.0 copy-start.2
  78.0 0.0 copy-start.3
  78.0 0.0 copy-start.4
  78.0 8.6 %fine.1 = (bf16[2,16,16,256]{3,2,1,0:T(8,128)(2,1)}, f32[16,16,256]{2,1,0:T(8,128)S(1)}, s32[16,128]{1,0:T(8,128)S(1)}) custom-call(s32[864]{0:T(1024)S(1)} %pad_add_fusion.idx_ref, s32[2,1]{1,0:T(2,128)S(1)} %copy.31.counts_ref, bf16[128,136,128]{2,1,0:T(8,128)(2,1)} %all-to-all-done.arrived_ref, bf16[2,16,16,256]{3,2,1,0:T(8,128)(2,1)S(1)} %copy-done.1, ...), custom_call_target="tpu_custom_call" | custom-call | flops 10000000000 | bytes 6000000 | tf_op jit(solution)/shard_map/fine/pallas_call | solution.py:431
  86.7 10.3 %all-to-all-done.1 = bf16[128,32,128]{2,1,0:T(8,128)(2,1)S(1)} async-done(((bf16[128,32,128]{2,1,0:T(8,128)(2,1)}), bf16[128,32,128]{2,1,0:T(8,128)(2,1)S(1)}, u32[]{:S(2)}, u32[]{:S(2)}) %all-to-all-start.1) | async-done | bytes 1048608 | tf_op jit(solution)/shard_map/all_to_all | solution.py:395
  97.0 0.0 copy-done.2
  97.0 0.0 copy-done.3
  97.0 0.0 copy-done.4
  97.0 5.8 %tail.1 = (bf16[2,16,16,256]{3,2,1,0:T(8,128)(2,1)}, bf16[1,16,256]{2,1,0:T(8,128)(2,1)}) custom-call(s32[16,128]{1,0:T(8,128)S(1)} %get-tuple-element.8.idx_ref, s32[16]{0:T(128)S(1)} %copy-done.3, s32[16]{0:T(128)S(1)} %copy-done.4, bf16[64,2,4,8,128]{4,3,2,1,0:T(8,128)(2,1)S(1)} %bitcast.90, ...), custom_call_target="tpu_custom_call", output_to_operand_aliasing={{0}: (9, {})} | custom-call | tf_op jit(solution)/shard_map/tail/pallas_call | solution.py:451
  (19 shorter events, 0.1 us)
Async XLA Ops:
  0.6 17.6 %copy-start = (bf16[3,4,3,16,16]{4,3,2,1,0:T(8,128)(2,1)S(1)}, bf16[3,4,3,16,16]{4,3,2,1,0:T(8,128)(2,1)}, u32[]{:S(2)}) copy-start(bf16[3,4,3,16,16]{4,3,2,1,0:T(8,128)(2,1)} %param.28) | copy-start | bytes 55300
  4.4 12.0 %copy-start.7 = (s32[2,16,16]{2,1,0:T(8,128)S(1)}, s32[2,16,16]{2,1,0:T(8,128)}, u32[]{:S(2)}) copy-start(s32[2,16,16]{2,1,0:T(8,128)} %param.19) | copy-start | bytes 6148
  4.4 12.0 %copy-start.8 = (s32[2,16,16]{2,1,0:T(8,128)S(1)}, s32[2,16,16]{2,1,0:T(8,128)}, u32[]{:S(2)}) copy-start(s32[2,16,16]{2,1,0:T(8,128)} %param.17) | copy-start | bytes 6148
  4.4 12.0 %copy-start.9 = (s32[2,16,16]{2,1,0:T(8,128)S(1)}, s32[2,16,16]{2,1,0:T(8,128)}, u32[]{:S(2)}) copy-start(s32[2,16,16]{2,1,0:T(8,128)} %param.18) | copy-start | bytes 6148
  4.4 12.5 %copy-start.10 = (s32[2,1]{0,1:T(1,128)S(1)}, s32[2,1]{0,1:T(1,128)}, u32[]{:S(2)}) copy-start(s32[2,1]{0,1:T(1,128)} %param.16) | copy-start | bytes 28
  4.4 12.6 %copy-start.6 = (bf16[3,4,3,16,16]{4,3,2,1,0:T(8,128)(2,1)S(1)}, bf16[3,4,3,16,16]{4,3,2,1,0:T(8,128)(2,1)}, u32[]{:S(2)}) copy-start(bf16[3,4,3,16,16]{4,3,2,1,0:T(8,128)(2,1)} %param.26) | copy-start | bytes 55300
  4.4 14.1 %copy-start.5 = (bf16[3,4,3,16,16]{4,3,2,1,0:T(8,128)(2,1)S(1)}, bf16[3,4,3,16,16]{4,3,2,1,0:T(8,128)(2,1)}, u32[]{:S(2)}) copy-start(bf16[3,4,3,16,16]{4,3,2,1,0:T(8,128)(2,1)} %param.27) | copy-start | bytes 55300
  4.4 66.9 %all-to-all-start = ((bf16[128,136,128]{2,1,0:T(8,128)(2,1)}), bf16[128,136,128]{2,1,0:T(8,128)(2,1)}, u32[]{:S(2)}, u32[]{:S(2)}) async-start(bf16[128,136,128]{2,1,0:T(8,128)(2,1)} %send.1), calls=%async_computation | async-start | bytes 8912896 | tf_op jit(solution)/shard_map/all_to_all | solution.py:381
  18.0 60.1 %copy-start.1 = (bf16[2,16,16,256]{3,2,1,0:T(8,128)(2,1)S(1)}, bf16[2,16,16,256]{3,2,1,0:T(8,128)(2,1)}, u32[]{:S(2)}) copy-start(bf16[2,16,16,256]{3,2,1,0:T(8,128)(2,1)} %fine_ref.3) | copy-start | bytes 786436
  73.4 23.6 %all-to-all-start.1 = ((bf16[128,32,128]{2,1,0:T(8,128)(2,1)}), bf16[128,32,128]{2,1,0:T(8,128)(2,1)S(1)}, u32[]{:S(2)}, u32[]{:S(2)}) async-start(bf16[128,32,128]{2,1,0:T(8,128)(2,1)} %get-tuple-element.9), calls=%async_computation.1 | async-start | bytes 2097152 | tf_op jit(solution)/shard_map/all_to_all | solution.py:395
  78.0 18.9 %copy-start.2 = (bf16[2,16,16]{2,1,0:T(8,128)(2,1)S(1)}, bf16[2,16,16]{2,1,0:T(8,128)(2,1)}, u32[]{:S(2)}) copy-start(bf16[2,16,16]{2,1,0:T(8,128)(2,1)} %filt_ref.3) | copy-start | bytes 3076
  78.0 18.9 %copy-start.3 = (s32[16]{0:T(128)S(1)}, s32[16]{0:T(128)}, u32[]{:S(2)}) copy-start(s32[16]{0:T(128)} %parent_ref.3) | copy-start | bytes 196
  78.0 18.9 %copy-start.4 = (s32[16]{0:T(128)S(1)}, s32[16]{0:T(128)}, u32[]{:S(2)}) copy-start(s32[16]{0:T(128)} %code_ref.3) | copy-start | bytes 196

commit v4 on v3

--- a/solution.py
+++ b/solution.py
@@ -14,7 +14,7 @@
 GROUP = 4
 BF = jnp.bfloat16
 F32 = jnp.float32
-AXES = ("grp", "lane")
+AXES = ("y", "core", "lane")
 
 
 def iota(shape, dim):
@@ -106,7 +106,7 @@
         rows.append(jnp.where(lane_block == b, chosen, 0.0).astype(BF))
     lifted = dot(jnp.concatenate(rows, axis=0), fine_ref[1].reshape(SLOT * K, KK)).astype(BF)
     moved = dot(corner_spread(lifted, code_ref), corner_tables(rep_t, tile_t))
-    parity = lax.axis_index("grp") % 2
+    parity = lax.axis_index("core")
     info = jnp.concatenate([refs_ref[...], codes_ref[...]] + [mask_ref[...]] * 6, axis=0)
     wide = (iota((16, 128), 0) == iota((16, 128), 1)).astype(BF)
     info = dot(info.astype(F32).astype(BF), wide).astype(BF)
@@ -133,8 +133,7 @@
 
 
 def place_kernel(arrived_ref, out_ref, info_ref, piece_ref, sem):
-    grp = lax.axis_index("grp")
-    parity = grp % 2
+    parity = lax.axis_index("core")
     copy = pltpu.make_async_copy(arrived_ref.at[:, :, :, pl.ds(128, 8)], piece_ref, sem)
     copy.start()
     copy.wait()
@@ -145,9 +144,9 @@
             total = total + piece_ref[g, 1 - parity, lane].astype(F32)
         sums.append(total)
     mine = jnp.concatenate(sums, axis=0).astype(BF)
-    for r in range(128):
+    for r in range(64):
         out_ref[r] = mine
-    info_ref[...] = piece_ref[grp // 2, parity]
+    info_ref[...] = piece_ref[lax.axis_index("y"), parity]
 
 
 def apply_level(level, blocks, place, xbd_ref, yw_ref, zw_ref, spread_ref, table_ref, acc_ref):
@@ -257,6 +256,7 @@
     parent_ref,
     code_ref,
     summed_ref,
+    other_ref,
     one_ref,
     xbd_ref,
     yw_ref,
@@ -274,13 +274,15 @@
     sems,
 ):
     copies = []
-    for g in range(8):
-        copies.append(
-            pltpu.make_async_copy(
-                summed_ref.at[:, 1 - g % 2, g // 2], pool_ref.at[g], sems.at[g]
+    parity = lax.axis_index("core")
+    for gp in range(4):
+        for ref, side in ((summed_ref, 1 - parity), (other_ref, parity)):
+            copies.append(
+                pltpu.make_async_copy(
+                    ref.at[:, gp], pool_ref.at[2 * gp + side], sems.at[len(copies)]
+                )
             )
-        )
-        copies[-1].start()
+            copies[-1].start()
     pool_ref[8, 0:4] = jnp.zeros((4, 8, 128), BF)
     blocks = pool_ref.reshape(9 * 512, 128)
     for copy in copies:
@@ -385,14 +387,14 @@
         in_specs=[anywhere()],
         out_specs=[vmem(), vmem()],
         out_shape=[
-            jax.ShapeDtypeStruct((128, 32, 128), BF),
+            jax.ShapeDtypeStruct((64, 32, 128), BF),
             jax.ShapeDtypeStruct((16, 8, 128), BF),
         ],
         scratch_shapes=[pltpu.VMEM((4, 2, 16, 8, 128), BF), pltpu.SemaphoreType.DMA],
         compiler_params=room(8),
         name="place",
     )(arrived.reshape(4, 2, 16, 136, 128))
-    summed = lax.all_to_all(summed, AXES[::-1], split_axis=0, concat_axis=0, tiled=True)
+    summed = lax.all_to_all(summed, ("lane", "y"), split_axis=0, concat_axis=0, tiled=True)
 
     repeat, tiled = spreads()
     yw = jnp.einsum("lmcpr,pk->lmcrk", ops_y, repeat, preferred_element_type=F32)
@@ -448,9 +450,11 @@
         ),
     )(idx, counts, arrived, fine_in, info, xbd, yw, zw)
 
+    summed, coarse_idx = lax.optimization_barrier((summed, coarse_idx))
+    other = lax.ppermute(summed, "core", [(0, 1), (1, 0)])
     fine_out, coarse_out = pl.pallas_call(
         tail_kernel,
-        in_specs=[smem()] * 3 + [anywhere()] + [vmem()] * 5 + [anywhere()],
+        in_specs=[smem()] * 3 + [anywhere()] * 2 + [vmem()] * 5 + [anywhere()],
         out_specs=[anywhere(), vmem()],
         out_shape=[
             jax.ShapeDtypeStruct((2, SLOT, K, KK), BF),
@@ -463,14 +467,15 @@
             pltpu.VMEM((SLOT, K, KK), BF),
             pltpu.SemaphoreType.DMA((9,)),
         ],
-        input_output_aliases={9: 0},
+        input_output_aliases={10: 0},
         compiler_params=room(16),
         name="tail",
     )(
         coarse_idx,
         parent_of,
         child_code,
-        summed.reshape(64, 2, 4, 8, 128),
+        summed.reshape(64, 4, 8, 128),
+        other.reshape(64, 4, 8, 128),
         one,
         xbd,
         yw,
@@ -502,4 +507,6 @@
         P(),
     )
     out_specs = (blocks, P(AXES, None, None))
+    parts = (mesh.shape["grp"] // 2, 2, mesh.shape["lane"])
+    mesh = jax.sharding.Mesh(mesh.devices.reshape(parts), AXES)
     return jax.shard_map(body, mesh=mesh, in_specs=in_specs, out_specs=out_specs, check_vma=False)

time: 103 us -> 99.8 us (0.969)
  waiting for transfers between devices: 62.7 us -> 56.7 us
  starting transfers between devices: 16.5 us -> 19.2 us
    all_to_all x1, waiting for transfers between devices: 10.3 us -> 2.77 us  [body(): lax.all_to_all(summed, ('lane', 'y'), split_axis=0, concat_axis=0, tiled=...]
    ppermute x0 -> x1, starting transfers between devices: none -> 2.48 us  [body(): other = lax.ppermute(summed, 'core', [(0, 1), (1, 0)])]
    ppermute x0 -> x1, waiting for transfers between devices: none -> 1.54 us  [body(): other = lax.ppermute(summed, 'core', [(0, 1), (1, 0)])]
  transfers between devices with their start and end apart: 2 -> 3, of which waited for: 2 -> 3; matrix products, arithmetic and copies ran while one was open for 2% -> 2% of each run, Pallas kernels for 8% -> 9%
where the time goes in v4:
time: 99.8 us; the launch traced here: 99.5 us
  waiting for transfers between devices  56.7 us (57%)
  Pallas kernels  20 us (20%)
  starting transfers between devices  19.2 us (19%)
  between operations  1.16 us (1%)
  matrix products  1.12 us (1%)
    all_to_all x1, waiting for transfers between devices, body(): lax.all_to_all(send, AXES, split_axis=0, concat_axis=0, tiled=True)  52.4 us
    all_to_all x1, starting transfers between devices, body(): lax.all_to_all(send, AXES, split_axis=0, concat_axis=0, tiled=True)  11.9 us
    pallas_call x1, Pallas kernels, body(): pl.pallas_call(fine_kernel, in_specs=[smem()] * 2 + [anywhere()] + [vmem(...  8.74 us
    pallas_call x1, Pallas kernels, body(): pl.pallas_call(tail_kernel, in_specs=[smem()] * 3 + [anywhere()] * 2 + [v...  5.74 us
    all_to_all x1, starting transfers between devices, body(): lax.all_to_all(summed, ('lane', 'y'), split_axis=0, concat_axis=0, tiled=...  4.8 us
    pallas_call x1, Pallas kernels, body(): pl.pallas_call(send_kernel, in_specs=[smem()] * 3 + [vmem()] * 5, out_spe...  3.73 us
    all_to_all x1, waiting for transfers between devices, body(): lax.all_to_all(summed, ('lane', 'y'), split_axis=0, concat_axis=0, tiled=...  2.77 us
    ppermute x1, starting transfers between devices, body(): other = lax.ppermute(summed, 'core', [(0, 1), (1, 0)])  2.48 us
  transfers between devices with their start and end apart: 3, of which 3 were waited for; matrix products, arithmetic and copies ran while one was open for 2% of the time, Pallas kernels for 9%

profile of v4, /device:TPU:1, one launch (start us, length us, event | category | flops | bytes accessed | tf_op | source)
XLA Modules:
  0.0 99.5 jit_solution(10257661861047431120)
XLA Ops:
  0.6 0.0 copy-start
  0.6 3.7 %send.1 = bf16[128,136,128]{2,1,0:T(8,128)(2,1)} custom-call(s32[16]{0:T(128)} %parent_ref.3, s32[16]{0:T(128)} %code_ref.3, s32[2,1,256]{2,1,0:T(1,128)} %slots_ref.1, bf16[2,16,16,256]{3,2,1,0:T(8,128)(2,1)} %fine_ref.3, bf16[2,16,16]{2,1,0:T(8,128)(2,1)} %filt_ref.3, s32[1,16]{1,0:T(1,128)} %refs_ref.1, s32[1,16]{1,0:T(1,128)} %codes_ref.1, s32[1,16]{1,0:T(1,128)} %mask_ref.1), custom_call_target="tpu_custom_call" | custom-call | tf_op jit(solution)/shard_map/send/pallas_call | solution.py:361
  4.4 0.0 copy-start.7
  4.4 0.0 copy-start.8
  4.4 0.0 copy-start.9
  4.4 0.0 copy-start.10
  4.4 0.0 copy-start.6
  4.4 0.0 copy-start.5
  4.5 11.9 %all-to-all-start = ((bf16[128,136,128]{2,1,0:T(8,128)(2,1)}), bf16[128,136,128]{2,1,0:T(8,128)(2,1)}, u32[]{:S(2)}, u32[]{:S(2)}) async-start(bf16[128,136,128]{2,1,0:T(8,128)(2,1)} %send.1), calls=%async_computation | async-start | bytes 8912896 | tf_op jit(solution)/shard_map/all_to_all | solution.py:383
  16.4 0.0 copy-done.7
  16.4 0.0 copy-done.8
  16.5 0.0 copy-done.9
  16.5 0.0 copy-start.1
  16.5 0.3 select_reduce_fusion
  16.8 0.1 add.171
  16.9 0.1 add.163
  17.0 0.0 copy-done.10
  17.0 0.1 copy.31.counts_ref
  17.1 0.0 copy-done.6
  17.1 0.1 copy.27
  17.2 0.1 reshape.256
  17.6 0.1 pad_add_fusion.idx_ref
  17.6 0.2 fusion.1
  17.8 0.3 fusion.9
  18.1 0.3 convolution_select_fusion.xbd_ref
  18.4 0.0 copy-done
  18.4 0.3 fusion.32
  18.7 0.0 copy-done.5
  18.7 0.3 fusion.29
  19.0 52.4 %all-to-all-done.arrived_ref = bf16[128,136,128]{2,1,0:T(8,128)(2,1)} async-done(((bf16[128,136,128]{2,1,0:T(8,128)(2,1)}), bf16[128,136,128]{2,1,0:T(8,128)(2,1)}, u32[]{:S(2)}, u32[]{:S(2)}) %all-to-all-start) | async-done | bytes 4456480 | tf_op jit(solution)/shard_map/all_to_all | solution.py:383
  71.4 1.8 %place.1 = (bf16[64,32,128]{2,1,0:T(8,128)(2,1)}, bf16[16,8,128]{2,1,0:T(8,128)(2,1)S(1)}) custom-call(bf16[4,2,16,136,128]{4,3,2,1,0:T(8,128)(2,1)} %bitcast.arrived_ref), custom_call_target="tpu_custom_call" | custom-call | tf_op jit(solution)/shard_map/place/pallas_call | solution.py:385
  73.2 4.8 %all-to-all-start.1 = ((bf16[64,32,128]{2,1,0:T(8,128)(2,1)}), bf16[64,32,128]{2,1,0:T(8,128)(2,1)S(1)}, u32[]{:S(2)}, u32[]{:S(2)}) async-start(bf16[64,32,128]{2,1,0:T(8,128)(2,1)} %get-tuple-element.9), calls=%async_computation.1 | async-start | bytes 1048576 | tf_op jit(solution)/shard_map/all_to_all | solution.py:397
  78.0 0.0 copy-done.1
  78.0 0.0 copy-start.2
  78.0 0.0 copy-start.3
  78.0 0.0 copy-start.4
  78.0 8.7 %fine.1 = (bf16[2,16,16,256]{3,2,1,0:T(8,128)(2,1)}, f32[16,16,256]{2,1,0:T(8,128)S(1)}, s32[16,128]{1,0:T(8,128)S(1)}) custom-call(s32[864]{0:T(1024)S(1)} %pad_add_fusion.idx_ref, s32[2,1]{1,0:T(2,128)S(1)} %copy.31.counts_ref, bf16[128,136,128]{2,1,0:T(8,128)(2,1)} %all-to-all-done.arrived_ref, bf16[2,16,16,256]{3,2,1,0:T(8,128)(2,1)S(1)} %copy-done.1, ...), custom_call_target="tpu_custom_call" | custom-call | flops 10000000000 | bytes 6000000 | tf_op jit(solution)/shard_map/fine/pallas_call | solution.py:433
  86.8 2.8 %all-to-all-done.1 = bf16[64,32,128]{2,1,0:T(8,128)(2,1)S(1)} async-done(((bf16[64,32,128]{2,1,0:T(8,128)(2,1)}), bf16[64,32,128]{2,1,0:T(8,128)(2,1)S(1)}, u32[]{:S(2)}, u32[]{:S(2)}) %all-to-all-start.1) | async-done | bytes 524320 | tf_op jit(solution)/shard_map/all_to_all | solution.py:397
  89.6 2.5 %collective-permute-start = (bf16[64,32,128]{2,1,0:T(8,128)(2,1)S(1)}, bf16[64,32,128]{2,1,0:T(8,128)(2,1)S(1)}, u32[]{:S(2)}, u32[]{:S(2)}) collective-permute-start(bf16[64,32,128]{2,1,0:T(8,128)(2,1)S(1)} %all-to-all-done.1), channel_id=1, source_target_pairs={{0,16},{16,0},{1,17},{17,1},{2,18},{18,2},{3,19},{19,3},{4,20},{20... | collective-permute-start | bytes 1572872 | tf_op jit(solution)/shard_map/ppermute | solution.py:454
  92.0 1.5 %collective-permute-done = bf16[64,32,128]{2,1,0:T(8,128)(2,1)S(1)} collective-permute-done((bf16[64,32,128]{2,1,0:T(8,128)(2,1)S(1)}, bf16[64,32,128]{2,1,0:T(8,128)(2,1)S(1)}, u32[]{:S(2)}, u32[]{:S(2)}) %collective-permute-start) | collective-permute-done | bytes 524320 | tf_op jit(solution)/shard_map/ppermute | solution.py:454
  93.6 0.0 copy-done.2
  93.6 0.0 copy-done.3
  93.6 0.0 copy-done.4
  93.6 5.7 %tail.1 = (bf16[2,16,16,256]{3,2,1,0:T(8,128)(2,1)}, bf16[1,16,256]{2,1,0:T(8,128)(2,1)}) custom-call(s32[16,128]{1,0:T(8,128)S(1)} %get-tuple-element.12.idx_ref, s32[16]{0:T(128)S(1)} %copy-done.3, s32[16]{0:T(128)S(1)} %copy-done.4, bf16[64,4,8,128]{3,2,1,0:T(8,128)(2,1)S(1)} %bitcast.95, ...), custom_call_target="tpu_custom_call", output_to_operand_aliasing={{0}: (10, {})} | custom-call | tf_op jit(solution)/shard_map/tail/pallas_call | solution.py:455
  (19 shorter events, 0.1 us)
Async XLA Ops:
  0.6 17.8 %copy-start = (bf16[3,4,3,16,16]{4,3,2,1,0:T(8,128)(2,1)S(1)}, bf16[3,4,3,16,16]{4,3,2,1,0:T(8,128)(2,1)}, u32[]{:S(2)}) copy-start(bf16[3,4,3,16,16]{4,3,2,1,0:T(8,128)(2,1)} %param.28) | copy-start | bytes 55300
  4.4 12.0 %copy-start.7 = (s32[2,16,16]{2,1,0:T(8,128)S(1)}, s32[2,16,16]{2,1,0:T(8,128)}, u32[]{:S(2)}) copy-start(s32[2,16,16]{2,1,0:T(8,128)} %param.19) | copy-start | bytes 6148
  4.4 12.0 %copy-start.8 = (s32[2,16,16]{2,1,0:T(8,128)S(1)}, s32[2,16,16]{2,1,0:T(8,128)}, u32[]{:S(2)}) copy-start(s32[2,16,16]{2,1,0:T(8,128)} %param.17) | copy-start | bytes 6148
  4.4 12.1 %copy-start.9 = (s32[2,16,16]{2,1,0:T(8,128)S(1)}, s32[2,16,16]{2,1,0:T(8,128)}, u32[]{:S(2)}) copy-start(s32[2,16,16]{2,1,0:T(8,128)} %param.18) | copy-start | bytes 6148
  4.4 12.6 %copy-start.10 = (s32[2,1]{0,1:T(1,128)S(1)}, s32[2,1]{0,1:T(1,128)}, u32[]{:S(2)}) copy-start(s32[2,1]{0,1:T(1,128)} %param.16) | copy-start | bytes 28
  4.4 12.7 %copy-start.6 = (bf16[3,4,3,16,16]{4,3,2,1,0:T(8,128)(2,1)S(1)}, bf16[3,4,3,16,16]{4,3,2,1,0:T(8,128)(2,1)}, u32[]{:S(2)}) copy-start(bf16[3,4,3,16,16]{4,3,2,1,0:T(8,128)(2,1)} %param.26) | copy-start | bytes 55300
  4.4 14.3 %copy-start.5 = (bf16[3,4,3,16,16]{4,3,2,1,0:T(8,128)(2,1)S(1)}, bf16[3,4,3,16,16]{4,3,2,1,0:T(8,128)(2,1)}, u32[]{:S(2)}) copy-start(bf16[3,4,3,16,16]{4,3,2,1,0:T(8,128)(2,1)} %param.27) | copy-start | bytes 55300
  4.5 66.9 %all-to-all-start = ((bf16[128,136,128]{2,1,0:T(8,128)(2,1)}), bf16[128,136,128]{2,1,0:T(8,128)(2,1)}, u32[]{:S(2)}, u32[]{:S(2)}) async-start(bf16[128,136,128]{2,1,0:T(8,128)(2,1)} %send.1), calls=%async_computation | async-start | bytes 8912896 | tf_op jit(solution)/shard_map/all_to_all | solution.py:383
  16.5 61.5 %copy-start.1 = (bf16[2,16,16,256]{3,2,1,0:T(8,128)(2,1)S(1)}, bf16[2,16,16,256]{3,2,1,0:T(8,128)(2,1)}, u32[]{:S(2)}) copy-start(bf16[2,16,16,256]{3,2,1,0:T(8,128)(2,1)} %fine_ref.3) | copy-start | bytes 786436
  73.2 16.4 %all-to-all-start.1 = ((bf16[64,32,128]{2,1,0:T(8,128)(2,1)}), bf16[64,32,128]{2,1,0:T(8,128)(2,1)S(1)}, u32[]{:S(2)}, u32[]{:S(2)}) async-start(bf16[64,32,128]{2,1,0:T(8,128)(2,1)} %get-tuple-element.9), calls=%async_computation.1 | async-start | bytes 1048576 | tf_op jit(solution)/shard_map/all_to_all | solution.py:397
  78.0 15.6 %copy-start.2 = (bf16[2,16,16]{2,1,0:T(8,128)(2,1)S(1)}, bf16[2,16,16]{2,1,0:T(8,128)(2,1)}, u32[]{:S(2)}) copy-start(bf16[2,16,16]{2,1,0:T(8,128)(2,1)} %filt_ref.3) | copy-start | bytes 3076
  78.0 15.6 %copy-start.3 = (s32[16]{0:T(128)S(1)}, s32[16]{0:T(128)}, u32[]{:S(2)}) copy-start(s32[16]{0:T(128)} %parent_ref.3) | copy-start | bytes 196
  78.0 15.6 %copy-start.4 = (s32[16]{0:T(128)S(1)}, s32[16]{0:T(128)}, u32[]{:S(2)}) copy-start(s32[16]{0:T(128)} %code_ref.3) | copy-start | bytes 196
  89.6 4.0 %collective-permute-start = (bf16[64,32,128]{2,1,0:T(8,128)(2,1)S(1)}, bf16[64,32,128]{2,1,0:T(8,128)(2,1)S(1)}, u32[]{:S(2)}, u32[]{:S(2)}) collective-permute-start(bf16[64,32,128]{2,1,0:T(8,128)(2,1)S(1)} %all-to-all-done.1), channel_id=1, source_target_pairs={{0,16},{16,0},{1,17},{17,1},{2,18},{18,2},{3,19},{19,3},{4,20},{20... | collective-permute-start | bytes 1572872 | tf_op jit(solution)/shard_map/ppermute | solution.py:454

commit v5 on v4

--- a/solution.py
+++ b/solution.py
@@ -132,21 +132,34 @@
         copy.wait()
 
 
-def place_kernel(arrived_ref, out_ref, info_ref, piece_ref, sem):
+def place_kernel(arrived_ref, out_ref, info_ref, piece_ref, copies_ref, sems):
     parity = lax.axis_index("core")
-    copy = pltpu.make_async_copy(arrived_ref.at[:, :, :, pl.ds(128, 8)], piece_ref, sem)
-    copy.start()
-    copy.wait()
+    tile = pl.ds(128, 8)
+    pieces = pltpu.make_async_copy(arrived_ref.at[:, 1 - parity, :, tile], piece_ref, sems.at[0])
+    pieces.start()
+    lists = pltpu.make_async_copy(
+        arrived_ref.at[lax.axis_index("y"), parity, :, tile], info_ref, sems.at[1]
+    )
+    lists.start()
+    pieces.wait()
     sums = []
     for g in range(4):
-        total = piece_ref[g, 1 - parity, 0].astype(F32)
+        total = piece_ref[g, 0].astype(F32)
         for lane in range(1, 16):
-            total = total + piece_ref[g, 1 - parity, lane].astype(F32)
+            total = total + piece_ref[g, lane].astype(F32)
         sums.append(total)
     mine = jnp.concatenate(sums, axis=0).astype(BF)
-    for r in range(64):
-        out_ref[r] = mine
-    info_ref[...] = piece_ref[lax.axis_index("y"), parity]
+    for r in range(16):
+        copies_ref[r] = mine
+    sends = [
+        pltpu.make_async_copy(copies_ref, out_ref.at[pl.ds(16 * i, 16)], sems.at[2 + i])
+        for i in range(4)
+    ]
+    for send in sends:
+        send.start()
+    lists.wait()
+    for send in sends:
+        send.wait()
 
 
 def apply_level(level, blocks, place, xbd_ref, yw_ref, zw_ref, spread_ref, table_ref, acc_ref):
@@ -385,12 +398,16 @@
     summed, info = pl.pallas_call(
         place_kernel,
         in_specs=[anywhere()],
-        out_specs=[vmem(), vmem()],
+        out_specs=[anywhere(), vmem()],
         out_shape=[
             jax.ShapeDtypeStruct((64, 32, 128), BF),
             jax.ShapeDtypeStruct((16, 8, 128), BF),
         ],
-        scratch_shapes=[pltpu.VMEM((4, 2, 16, 8, 128), BF), pltpu.SemaphoreType.DMA],
+        scratch_shapes=[
+            pltpu.VMEM((4, 16, 8, 128), BF),
+            pltpu.VMEM((16, 32, 128), BF),
+            pltpu.SemaphoreType.DMA((6,)),
+        ],
         compiler_params=room(8),
         name="place",
     )(arrived.reshape(4, 2, 16, 136, 128))

time: 99.8 us -> 99.8 us (level)
  no operation moved by 1% of the time
where the time goes in v5:
time: 99.8 us; the launch traced here: 99.5 us
  waiting for transfers between devices  56.7 us (57%)
  Pallas kernels  20 us (20%)
  starting transfers between devices  19.2 us (19%)
  between operations  1.16 us (1%)
  matrix products  1.12 us (1%)
    all_to_all x1, waiting for transfers between devices, body(): lax.all_to_all(send, AXES, split_axis=0, concat_axis=0, tiled=True)  52.4 us
    all_to_all x1, starting transfers between devices, body(): lax.all_to_all(send, AXES, split_axis=0, concat_axis=0, tiled=True)  11.9 us
    pallas_call x1, Pallas kernels, body(): pl.pallas_call(fine_kernel, in_specs=[smem()] * 2 + [anywhere()] + [vmem(...  8.74 us
    pallas_call x1, Pallas kernels, body(): pl.pallas_call(tail_kernel, in_specs=[smem()] * 3 + [anywhere()] * 2 + [v...  5.74 us
    all_to_all x1, starting transfers between devices, body(): lax.all_to_all(summed, ('lane', 'y'), split_axis=0, concat_axis=0, tiled=...  4.8 us
    pallas_call x1, Pallas kernels, body(): pl.pallas_call(send_kernel, in_specs=[smem()] * 3 + [vmem()] * 5, out_spe...  3.76 us
    all_to_all x1, waiting for transfers between devices, body(): lax.all_to_all(summed, ('lane', 'y'), split_axis=0, concat_axis=0, tiled=...  2.78 us
    ppermute x1, starting transfers between devices, body(): other = lax.ppermute(summed, 'core', [(0, 1), (1, 0)])  2.48 us
  transfers between devices with their start and end apart: 3, of which 3 were waited for; matrix products, arithmetic and copies ran while one was open for 2% of the time, Pallas kernels for 9%

profile of v5, /device:TPU:1, one launch (start us, length us, event | category | flops | bytes accessed | tf_op | source)
XLA Modules:
  0.0 99.5 jit_solution(12959629380640622068)
XLA Ops:
  0.6 0.0 copy-start
  0.6 3.8 %send.1 = bf16[128,136,128]{2,1,0:T(8,128)(2,1)} custom-call(s32[16]{0:T(128)} %parent_ref.3, s32[16]{0:T(128)} %code_ref.3, s32[2,1,256]{2,1,0:T(1,128)} %slots_ref.1, bf16[2,16,16,256]{3,2,1,0:T(8,128)(2,1)} %fine_ref.3, bf16[2,16,16]{2,1,0:T(8,128)(2,1)} %filt_ref.3, s32[1,16]{1,0:T(1,128)} %refs_ref.1, s32[1,16]{1,0:T(1,128)} %codes_ref.1, s32[1,16]{1,0:T(1,128)} %mask_ref.1), custom_call_target="tpu_custom_call" | custom-call | tf_op jit(solution)/shard_map/send/pallas_call | solution.py:374
  4.4 0.0 copy-start.7
  4.4 0.0 copy-start.8
  4.4 0.0 copy-start.9
  4.5 0.0 copy-start.10
  4.5 0.0 copy-start.6
  4.5 0.0 copy-start.5
  4.5 11.9 %all-to-all-start = ((bf16[128,136,128]{2,1,0:T(8,128)(2,1)}), bf16[128,136,128]{2,1,0:T(8,128)(2,1)}, u32[]{:S(2)}, u32[]{:S(2)}) async-start(bf16[128,136,128]{2,1,0:T(8,128)(2,1)} %send.1), calls=%async_computation | async-start | bytes 8912896 | tf_op jit(solution)/shard_map/all_to_all | solution.py:396
  16.4 0.0 copy-done.7
  16.4 0.0 copy-done.8
  16.5 0.0 copy-done.9
  16.5 0.0 copy-start.1
  16.5 0.3 select_reduce_fusion
  16.8 0.1 add.171
  16.9 0.1 add.163
  17.0 0.0 copy-done.10
  17.0 0.1 copy.31.counts_ref
  17.1 0.0 copy-done.6
  17.1 0.1 copy.27
  17.3 0.1 reshape.256
  17.6 0.1 pad_add_fusion.idx_ref
  17.6 0.2 fusion.1
  17.8 0.3 fusion.9
  18.1 0.3 convolution_select_fusion.xbd_ref
  18.4 0.0 copy-done
  18.4 0.3 fusion.32
  18.7 0.0 copy-done.5
  18.7 0.3 fusion.29
  19.0 52.4 %all-to-all-done.arrived_ref = bf16[128,136,128]{2,1,0:T(8,128)(2,1)} async-done(((bf16[128,136,128]{2,1,0:T(8,128)(2,1)}), bf16[128,136,128]{2,1,0:T(8,128)(2,1)}, u32[]{:S(2)}, u32[]{:S(2)}) %all-to-all-start) | async-done | bytes 4456480 | tf_op jit(solution)/shard_map/all_to_all | solution.py:396
  71.4 1.8 %place.1 = (bf16[64,32,128]{2,1,0:T(8,128)(2,1)}, bf16[16,8,128]{2,1,0:T(8,128)(2,1)S(1)}) custom-call(bf16[4,2,16,136,128]{4,3,2,1,0:T(8,128)(2,1)} %bitcast.arrived_ref), custom_call_target="tpu_custom_call" | custom-call | tf_op jit(solution)/shard_map/place/pallas_call | solution.py:398
  73.2 4.8 %all-to-all-start.1 = ((bf16[64,32,128]{2,1,0:T(8,128)(2,1)}), bf16[64,32,128]{2,1,0:T(8,128)(2,1)S(1)}, u32[]{:S(2)}, u32[]{:S(2)}) async-start(bf16[64,32,128]{2,1,0:T(8,128)(2,1)} %get-tuple-element.9), calls=%async_computation.1 | async-start | bytes 1048576 | tf_op jit(solution)/shard_map/all_to_all | solution.py:414
  78.0 0.0 copy-done.1
  78.0 0.0 copy-start.2
  78.0 0.0 copy-start.3
  78.0 0.0 copy-start.4
  78.0 8.7 %fine.1 = (bf16[2,16,16,256]{3,2,1,0:T(8,128)(2,1)}, f32[16,16,256]{2,1,0:T(8,128)S(1)}, s32[16,128]{1,0:T(8,128)S(1)}) custom-call(s32[864]{0:T(1024)S(1)} %pad_add_fusion.idx_ref, s32[2,1]{1,0:T(2,128)S(1)} %copy.31.counts_ref, bf16[128,136,128]{2,1,0:T(8,128)(2,1)} %all-to-all-done.arrived_ref, bf16[2,16,16,256]{3,2,1,0:T(8,128)(2,1)S(1)} %copy-done.1, ...), custom_call_target="tpu_custom_call" | custom-call | flops 10000000000 | bytes 6000000 | tf_op jit(solution)/shard_map/fine/pallas_call | solution.py:450
  86.8 2.8 %all-to-all-done.1 = bf16[64,32,128]{2,1,0:T(8,128)(2,1)S(1)} async-done(((bf16[64,32,128]{2,1,0:T(8,128)(2,1)}), bf16[64,32,128]{2,1,0:T(8,128)(2,1)S(1)}, u32[]{:S(2)}, u32[]{:S(2)}) %all-to-all-start.1) | async-done | bytes 524320 | tf_op jit(solution)/shard_map/all_to_all | solution.py:414
  89.5 2.5 %collective-permute-start = (bf16[64,32,128]{2,1,0:T(8,128)(2,1)S(1)}, bf16[64,32,128]{2,1,0:T(8,128)(2,1)S(1)}, u32[]{:S(2)}, u32[]{:S(2)}) collective-permute-start(bf16[64,32,128]{2,1,0:T(8,128)(2,1)S(1)} %all-to-all-done.1), channel_id=1, source_target_pairs={{0,16},{16,0},{1,17},{17,1},{2,18},{18,2},{3,19},{19,3},{4,20},{20... | collective-permute-start | bytes 1572872 | tf_op jit(solution)/shard_map/ppermute | solution.py:471
  92.0 1.5 %collective-permute-done = bf16[64,32,128]{2,1,0:T(8,128)(2,1)S(1)} collective-permute-done((bf16[64,32,128]{2,1,0:T(8,128)(2,1)S(1)}, bf16[64,32,128]{2,1,0:T(8,128)(2,1)S(1)}, u32[]{:S(2)}, u32[]{:S(2)}) %collective-permute-start) | collective-permute-done | bytes 524320 | tf_op jit(solution)/shard_map/ppermute | solution.py:471
  93.6 0.0 copy-done.2
  93.6 0.0 copy-done.3
  93.6 0.0 copy-done.4
  93.6 5.7 %tail.1 = (bf16[2,16,16,256]{3,2,1,0:T(8,128)(2,1)}, bf16[1,16,256]{2,1,0:T(8,128)(2,1)}) custom-call(s32[16,128]{1,0:T(8,128)S(1)} %get-tuple-element.12.idx_ref, s32[16]{0:T(128)S(1)} %copy-done.3, s32[16]{0:T(128)S(1)} %copy-done.4, bf16[64,4,8,128]{3,2,1,0:T(8,128)(2,1)S(1)} %bitcast.95, ...), custom_call_target="tpu_custom_call", output_to_operand_aliasing={{0}: (10, {})} | custom-call | tf_op jit(solution)/shard_map/tail/pallas_call | solution.py:472
  (19 shorter events, 0.1 us)
Async XLA Ops:
  0.6 17.8 %copy-start = (bf16[3,4,3,16,16]{4,3,2,1,0:T(8,128)(2,1)S(1)}, bf16[3,4,3,16,16]{4,3,2,1,0:T(8,128)(2,1)}, u32[]{:S(2)}) copy-start(bf16[3,4,3,16,16]{4,3,2,1,0:T(8,128)(2,1)} %param.28) | copy-start | bytes 55300
  4.4 12.0 %copy-start.7 = (s32[2,16,16]{2,1,0:T(8,128)S(1)}, s32[2,16,16]{2,1,0:T(8,128)}, u32[]{:S(2)}) copy-start(s32[2,16,16]{2,1,0:T(8,128)} %param.19) | copy-start | bytes 6148
  4.4 12.0 %copy-start.8 = (s32[2,16,16]{2,1,0:T(8,128)S(1)}, s32[2,16,16]{2,1,0:T(8,128)}, u32[]{:S(2)}) copy-start(s32[2,16,16]{2,1,0:T(8,128)} %param.17) | copy-start | bytes 6148
  4.4 12.0 %copy-start.9 = (s32[2,16,16]{2,1,0:T(8,128)S(1)}, s32[2,16,16]{2,1,0:T(8,128)}, u32[]{:S(2)}) copy-start(s32[2,16,16]{2,1,0:T(8,128)} %param.18) | copy-start | bytes 6148
  4.5 12.5 %copy-start.10 = (s32[2,1]{0,1:T(1,128)S(1)}, s32[2,1]{0,1:T(1,128)}, u32[]{:S(2)}) copy-start(s32[2,1]{0,1:T(1,128)} %param.16) | copy-start | bytes 28
  4.5 12.6 %copy-start.6 = (bf16[3,4,3,16,16]{4,3,2,1,0:T(8,128)(2,1)S(1)}, bf16[3,4,3,16,16]{4,3,2,1,0:T(8,128)(2,1)}, u32[]{:S(2)}) copy-start(bf16[3,4,3,16,16]{4,3,2,1,0:T(8,128)(2,1)} %param.26) | copy-start | bytes 55300
  4.5 14.2 %copy-start.5 = (bf16[3,4,3,16,16]{4,3,2,1,0:T(8,128)(2,1)S(1)}, bf16[3,4,3,16,16]{4,3,2,1,0:T(8,128)(2,1)}, u32[]{:S(2)}) copy-start(bf16[3,4,3,16,16]{4,3,2,1,0:T(8,128)(2,1)} %param.27) | copy-start | bytes 55300
  4.5 66.9 %all-to-all-start = ((bf16[128,136,128]{2,1,0:T(8,128)(2,1)}), bf16[128,136,128]{2,1,0:T(8,128)(2,1)}, u32[]{:S(2)}, u32[]{:S(2)}) async-start(bf16[128,136,128]{2,1,0:T(8,128)(2,1)} %send.1), calls=%async_computation | async-start | bytes 8912896 | tf_op jit(solution)/shard_map/all_to_all | solution.py:396
  16.5 61.5 %copy-start.1 = (bf16[2,16,16,256]{3,2,1,0:T(8,128)(2,1)S(1)}, bf16[2,16,16,256]{3,2,1,0:T(8,128)(2,1)}, u32[]{:S(2)}) copy-start(bf16[2,16,16,256]{3,2,1,0:T(8,128)(2,1)} %fine_ref.3) | copy-start | bytes 786436
  73.2 16.4 %all-to-all-start.1 = ((bf16[64,32,128]{2,1,0:T(8,128)(2,1)}), bf16[64,32,128]{2,1,0:T(8,128)(2,1)S(1)}, u32[]{:S(2)}, u32[]{:S(2)}) async-start(bf16[64,32,128]{2,1,0:T(8,128)(2,1)} %get-tuple-element.9), calls=%async_computation.1 | async-start | bytes 1048576 | tf_op jit(solution)/shard_map/all_to_all | solution.py:414
  78.0 15.6 %copy-start.2 = (bf16[2,16,16]{2,1,0:T(8,128)(2,1)S(1)}, bf16[2,16,16]{2,1,0:T(8,128)(2,1)}, u32[]{:S(2)}) copy-start(bf16[2,16,16]{2,1,0:T(8,128)(2,1)} %filt_ref.3) | copy-start | bytes 3076
  78.0 15.6 %copy-start.3 = (s32[16]{0:T(128)S(1)}, s32[16]{0:T(128)}, u32[]{:S(2)}) copy-start(s32[16]{0:T(128)} %parent_ref.3) | copy-start | bytes 196
  78.0 15.6 %copy-start.4 = (s32[16]{0:T(128)S(1)}, s32[16]{0:T(128)}, u32[]{:S(2)}) copy-start(s32[16]{0:T(128)} %code_ref.3) | copy-start | bytes 196
  89.5 4.0 %collective-permute-start = (bf16[64,32,128]{2,1,0:T(8,128)(2,1)S(1)}, bf16[64,32,128]{2,1,0:T(8,128)(2,1)S(1)}, u32[]{:S(2)}, u32[]{:S(2)}) collective-permute-start(bf16[64,32,128]{2,1,0:T(8,128)(2,1)S(1)} %all-to-all-done.1), channel_id=1, source_target_pairs={{0,16},{16,0},{1,17},{17,1},{2,18},{18,2},{3,19},{19,3},{4,20},{20... | collective-permute-start | bytes 1572872 | tf_op jit(solution)/shard_map/ppermute | solution.py:471
